TPU v7x, 128 devices: a whole 4x4x4 slice. The times are simulated.
128 devices in a mesh: dp: 8 (over x, core), fsdp: 16 (over y, z).
Axes of the slice: x: 4, y: 4, z: 4, core: 2. Of those that a mesh axis runs over, the one named last changes fastest.
Arguments:
- old_states: float32 [3, 2, 34816, 1792], P(None, None, ('dp', 'fsdp')), may hold values from -1.2 to 1.2, as said below
- old_bounds: int32 [8, 17], replicated, may hold values from 0 to 4096, as said below
- new_bounds: int32 [8, 17], replicated, may hold values from 0 to 4096, as said below
- failed: int32 [16], replicated, may hold values from 0 to 7, as said below
- tokens: bfloat16 [4096, 4096], P('fsdp'), may hold values from -6 to 6
- cotangent: bfloat16 [4096, 14336], P('fsdp', 'dp'), may hold values from -0.1875 to 0.1875
Outputs:
- new_states: float32 [3, 38912, 1792], P(None, ('dp', 'fsdp'))
- activations: bfloat16 [4096, 14336], P('fsdp', 'dp')
Inputs may be any that keep to these rules, and one draw needn't show every extreme that they name: Each row starts at 0, ends at 4096 and rises; old_bounds[g, f] is within 8 of f * 256, so each piece has 240 to 272 rows, and 272 is reached in every group. `new_bounds`: each row starts at 0 and ends at 4096; every entry is within 16 of the same entry of old_bounds, each piece has at most 304 rows, and 304 is reached in every group. `failed`: every group appears exactly 16 // 8 times. `old_states`: copy 0 of a failed device holds nothing of the states; the third state is positive.
All inputs are finite; a program needn't handle non-finite values.
Results may differ from a plain program's by a relative error of at most 0.018.
Values may be sent and summed in bfloat16 or wider, within the bound.
A program may use at most 192 MiB of HBM per device.

v0:
```python
import jax
import jax.numpy as jnp
from jax import lax
from jax.sharding import PartitionSpec as P

beta_one = 0.9
beta_two = 0.95
learn_rate = 0.01
decay_rate = 0.1
epsilon = 1e-08
correct_one = 1.0 - 0.9**8
correct_two = 1.0 - 0.95**8


def passed_along(value, axis, steps):
    count = lax.axis_size(axis)
    pairs = [(source, (source + steps) % count) for source in range(count)]
    return lax.ppermute(value, axis, pairs)


def extended_2(shard, sides, width):
    for axis, dim in sides:
        size, length = (lax.axis_size(axis), shard.shape[dim])
        up = [(i, (i + 1) % size) for i in range(size - 1)]
        down = [(j, i) for i, j in up]
        last = lax.slice_in_dim(shard, length - width, length, axis=dim)
        leading = lax.slice_in_dim(shard, 0, width, axis=dim)
        before = lax.ppermute(last, axis, up)
        after = lax.ppermute(leading, axis, down)
        shard = jnp.concatenate([before, shard, after], axis=dim)
    return shard


def pick_columns(tokens, bounds, row_count, capacity):
    flat_index = jnp.arange(row_count, dtype=jnp.int32)
    owner_ids = flat_index // capacity
    offsets = flat_index % capacity
    first_row = jnp.take(bounds, owner_ids)
    length = jnp.take(bounds, owner_ids + 1) - first_row
    target = jnp.minimum(first_row + offsets, tokens.shape[1] - 1)
    picked = jnp.take(tokens, target, axis=1)
    return jnp.where((offsets < length)[None, :], picked, jnp.zeros((), tokens.dtype))


def body(old_states, old_bounds, new_bounds, failed, tokens, cotangent):
    members = lax.axis_size("fsdp")
    my_group = lax.axis_index("dp")
    member_id = lax.axis_index("fsdp")
    lost_group = failed[member_id]
    rows_avg = tokens.shape[1] // members
    margin = rows_avg // 16
    cap_old = old_states.shape[2]
    cap_new = rows_avg + 3 * margin
    block_width = cotangent.shape[1]
    own_old = old_bounds[my_group]
    own_new = new_bounds[my_group]
    old_start = own_old[member_id]
    old_len = own_old[member_id + 1] - old_start
    new_start = own_new[member_id]
    new_len = own_new[member_id + 1] - new_start
    backup = old_states[:, 1]
    arrived = passed_along(backup.astype(jnp.bfloat16), "dp", 1).astype(backup.dtype)
    recovered = jnp.where(my_group == lost_group, arrived, old_states[:, 0])
    slot_old = jnp.arange(cap_old, dtype=jnp.int32)
    recovered = jnp.where(
        (slot_old < old_len)[None, :, None], recovered, jnp.zeros((), jnp.float32)
    )
    head_rows = recovered[:, :margin]
    tail_rows = lax.dynamic_slice_in_dim(recovered, old_len - margin, margin, 1)
    rim_rows = extended_2(
        jnp.concatenate([head_rows, tail_rows], 1).astype(jnp.bfloat16), (("fsdp", 1),), margin
    ).astype(jnp.float32)
    from_left = rim_rows[:, :margin]
    from_right = rim_rows[:, 3 * margin :]
    extended = jnp.zeros((3, margin + cap_old + margin + cap_new, block_width), jnp.float32)
    extended = lax.dynamic_update_slice_in_dim(extended, from_left, 0, 1)
    extended = lax.dynamic_update_slice_in_dim(extended, recovered, margin, 1)
    extended = lax.dynamic_update_slice_in_dim(extended, from_right, margin + old_len, 1)
    moved = lax.dynamic_slice_in_dim(extended, new_start - old_start + margin, cap_new, 1)
    slot_new = jnp.arange(cap_new, dtype=jnp.int32)
    moved = jnp.where((slot_new < new_len)[None, :, None], moved, jnp.zeros((), jnp.float32))
    block_rows = lax.all_gather(moved[0].astype(jnp.bfloat16), "fsdp", axis=0, tiled=True)
    picked = pick_columns(tokens, own_new, block_rows.shape[0], cap_new)
    hidden = jnp.dot(picked, block_rows, preferred_element_type=jnp.float32)
    activations = hidden.astype(jnp.bfloat16)
    picked = pick_columns(tokens, own_new, lax.axis_size("fsdp") * cap_new, cap_new)
    gradient = lax.psum_scatter(
        lax.dot_general(
            picked, cotangent, (((0,), (0,)), ((), ())), preferred_element_type=jnp.float32
        ).astype(jnp.bfloat16),
        "fsdp",
        scatter_dimension=0,
        tiled=True,
    ).astype(jnp.float32)
    weight = moved[0]
    moment_one = beta_one * moved[1] + (1.0 - beta_one) * gradient
    moment_two = beta_two * moved[2] + (1.0 - beta_two) * gradient * gradient
    update_dir = (
        moment_one / correct_one / (jnp.sqrt(moment_two / correct_two) + epsilon)
        + decay_rate * weight
    )
    new_weight = weight - learn_rate * update_dir
    return (jnp.stack([new_weight, moment_one, moment_two]), activations)


def solution(mesh):
    in_specs = (
        P(None, None, ("dp", "fsdp"), None),
        P(),
        P(),
        P(),
        P("fsdp", None),
        P("fsdp", "dp"),
    )
    out_specs = (P(None, ("dp", "fsdp"), None), P("fsdp", "dp"))
    return jax.shard_map(body, mesh=mesh, in_specs=in_specs, out_specs=out_specs, check_vma=False)
```

profile of v0, /device:TPU:0, one launch (start us, length us, event | category | flops | bytes accessed | tf_op | source)
XLA Modules:
  0.0 316.9 jit_solution(7382928010844779609)
XLA Ops:
  7.2 0.0 reduce-scatter.2.cloned.1.call-start
  7.2 0.8 fusion.17
  8.0 0.7 fusion.20
  8.7 10.8 %compare_select_fusion = s32[4864]{0:T(1024)S(1)} fusion(s32[]{:T(128)} %bitcast.26, s32[]{:T(128)} %bitcast.25, s32[]{:T(128)} %bitcast.24, s32[]{:T(128)} %bitcast.23, s32[]{:T(128)} %bitcast.22, s32[]{:T(128)} %bitcast.21, s32[]{:T(128)} %bitcast.20, s32[]{:T(128)} %bitcast.19, s32[]{:T(128)} %bitcast.18, s32[]{:T(128)} %bitcast.17, s32[]{:T(128)} %bitcast.16, ...), kind=kLoop, calls=%fused_computation.31 | loop fusion | flops 272384 | bytes 19524 | tf_op jit(solution)/shard_map/jit(_take)/jit(_where)/select_n | solution.py:41
  19.5 10.8 %fusion.12 = (pred[4864]{0:T(1024)(128)(4,1)S(1)}, pred[4864]{0:T(1024)(128)(4,1)S(1)}) fusion(s32[]{:T(128)} %bitcast.26, s32[]{:T(128)} %bitcast.25, s32[]{:T(128)} %bitcast.24, s32[]{:T(128)} %bitcast.23, s32[]{:T(128)} %bitcast.22, s32[]{:T(128)} %bitcast.21, s32[]{:T(128)} %bitcast.20, s32[]{:T(128)} %bitcast.19, s32[]{:T(128)} %bitcast.18, ...), kind=kLoop, calls=%fused_computation.42 | loop fusion | flops 491264 | bytes 9796 | tf_op jit(solution)/shard_map/lt | solution.py:42
  30.4 3.3 %copy.10 = bf16[256,4096]{0,1:T(8,128)(2,1)S(1)} copy(bf16[256,4096]{1,0:T(8,128)(2,1)} %param.14) | data formatting | bytes 4194304 | tf_op args[4]
  33.7 14.4 %gather_fusion = bf16[4864,256]{1,0:T(8,128)(2,1)} fusion(bf16[256,4096]{0,1:T(8,128)(2,1)S(1)} %copy.10, s32[5120]{0:T(1024)S(1)} %pad_clamp_fusion), kind=kCustom, calls=%fused_computation.clone | custom fusion | bytes 5000192 | tf_op jit(solution)/shard_map/jit(_take)/gather | solution.py:41
  48.1 11.7 %convolution_convert_fusion = bf16[4864,1792]{1,0:T(8,128)(2,1)} fusion(bf16[256,1792]{1,0:T(8,128)(2,1)S(1)} %copy-done, bf16[4864,256]{1,0:T(8,128)(2,1)} %gather_fusion, pred[4864]{0:T(1024)(128)(4,1)S(1)} %get-tuple-element.35, pred[4864]{0:T(1024)(128)(4,1)S(1)} %get-tuple-element.34), kind=kOutput, calls=%fused_computation.1 | convolution fusion | flops 4473946112 | bytes 20850176 | tf_op jit(solution)/shard_map/dot_general | solution.py:88
  59.8 0.0 all-gather.2.cloned.1.call-start
  59.8 4.5 %fusion.2 = bf16[3,272,1792]{2,1,0:T(8,128)(2,1)} fusion(f32[3,2,272,1792]{3,2,1,0:T(8,128)} %param.10), kind=kLoop, calls=%fused_computation.9 | loop fusion | bytes 5849088 | tf_op jit(solution)/shard_map/convert_element_type | solution.py:62
  64.4 0.6 dynamic_slice.29
  65.6 1.4 fusion.18
  68.3 31.9 %collective-permute-done = bf16[3,272,1792]{2,1,0:T(8,128)(2,1)} collective-permute-done((bf16[3,272,1792]{2,1,0:T(8,128)(2,1)}, bf16[3,272,1792]{2,1,0:T(8,128)(2,1)}, u32[]{:S(2)}, u32[]{:S(2)}) %collective-permute-start) | collective-permute-done | bytes 2924576 | tf_op jit(solution)/shard_map/ppermute | solution.py:18
  100.2 4.4 %fusion.1 = f32[3,272,1792]{2,1,0:T(8,128)S(1)} fusion(bf16[3,272,1792]{2,1,0:T(8,128)(2,1)} %collective-permute-done, pred[272]{0:T(512)(128)(4,1)S(1)} %iota_compare_fusion, pred[]{:T(512)S(6)} %eq.6, f32[3,2,272,1792]{3,2,1,0:T(8,128)} %param.10), kind=kLoop, calls=%fused_computation.6 | loop fusion | flops 4386816 | bytes 14622993 | tf_op jit(solution)/shard_map/jit(_where)/select_n | solution.py:65
  104.7 2.5 copy-done.3
  107.2 0.1 dynamic-slice_convert_fusion
  107.3 3.9 %collective-permute-start.1 = (bf16[3,16,1792]{2,1,0:T(8,128)(2,1)S(1)}, bf16[3,16,1792]{2,1,0:T(8,128)(2,1)S(1)}, u32[]{:S(2)}, u32[]{:S(2)}) collective-permute-start(bf16[3,16,1792]{2,1,0:T(8,128)(2,1)S(1)} %get-tuple-element.7), channel_id=1, source_target_pairs={{0,1},{1,2},{2,3},{3,4},{4,5},{5,6},{6,7},{7,8},{8,9},{9,10},{10,1... | collective-permute-start | bytes 516104 | tf_op jit(solution)/shard_map/ppermute | solution.py:28
  111.2 1.5 collective-permute-start.2
  115.2 3.3 %collective-permute-done.1 = bf16[3,16,1792]{2,1,0:T(8,128)(2,1)S(1)} collective-permute-done((bf16[3,16,1792]{2,1,0:T(8,128)(2,1)S(1)}, bf16[3,16,1792]{2,1,0:T(8,128)(2,1)S(1)}, u32[]{:S(2)}, u32[]{:S(2)}) %collective-permute-start.1) | collective-permute-done | bytes 172064 | tf_op jit(solution)/shard_map/ppermute | solution.py:28
  118.5 4.5 %collective-permute-done.2 = bf16[3,16,1792]{2,1,0:T(8,128)(2,1)S(1)} collective-permute-done((bf16[3,16,1792]{2,1,0:T(8,128)(2,1)S(1)}, bf16[3,16,1792]{2,1,0:T(8,128)(2,1)S(1)}, u32[]{:S(2)}, u32[]{:S(2)}) %collective-permute-start.2) | collective-permute-done | bytes 172064 | tf_op jit(solution)/shard_map/ppermute | solution.py:29
  123.0 0.1 fusion.10
  123.0 6.5 %dynamic_update_slice.9 = f32[3,608,1792]{2,1,0:T(8,128)} pad(f32[3,16,1792]{2,1,0:T(8,128)S(1)} %get-tuple-element.10, f32[]{:T(128)} %constant.130.clone.1), padding=0_0x0_592x0_0 | pad | bytes 13418500 | tf_op jit(solution)/shard_map/dynamic_update_slice | solution.py:76
  129.6 2.9 constant_dynamic-update-slice_fusion
  132.5 2.1 dynamic_update_slice.11
  134.6 3.7 %dynamic-slice_select_fusion = f32[3,304,1792]{2,1,0:T(8,128)S(1)} fusion(f32[3,608,1792]{2,1,0:T(8,128)} %dynamic_update_slice.11, s32[]{:T(128)S(6)} %select_n.94, pred[304]{0:T(512)(128)(4,1)S(1)} %iota_compare_fusion.1), kind=kLoop, calls=%fused_computation.3 | loop fusion | flops 1634304 | bytes 13074740 | tf_op jit(solution)/shard_map/jit(_where)/select_n | solution.py:81
  138.3 2.8 copy-done.2
  141.1 1.1 fusion.7
  142.2 38.2 %reduce-scatter.2.cloned.1.call-done = bf16[304,1792]{1,0:T(8,128)(2,1)} async-done(((bf16[4864,1792]{1,0:T(8,128)(2,1)}), bf16[304,1792]{1,0:T(8,128)(2,1)}) %reduce-scatter.2.cloned.1.call-update) | async-done | bytes 1089552 | tf_op jit(solution)/shard_map/reduce_scatter | solution.py:87
  180.4 4.9 %subtract_bitcast_fusion = (f32[1,304,1792]{2,1,0:T(8,128)S(1)}, f32[1,304,1792]{2,1,0:T(8,128)S(1)}, f32[1,304,1792]{2,1,0:T(8,128)S(1)}) fusion(f32[3,304,1792]{2,1,0:T(8,128)} %copy-done.2, bf16[304,1792]{1,0:T(8,128)(2,1)} %reduce-scatter.2.cloned.1.call-done), kind=kLoop, calls=%fused_computation.20 | loop fusion | flops 8716288 | bytes 14163968 | tf_op jit(solution)/shard_map/stack | solution.py:103
  185.3 3.2 %pad_maximum_fusion = f32[3,304,1792]{2,1,0:T(8,128)} fusion(f32[1,304,1792]{2,1,0:T(8,128)S(1)} %get-tuple-element.5, f32[1,304,1792]{2,1,0:T(8,128)S(1)} %get-tuple-element.6, f32[1,304,1792]{2,1,0:T(8,128)S(1)} %get-tuple-element.4), kind=kLoop, calls=%fused_computation.2 | loop fusion | flops 3268608 | bytes 13074432 | tf_op jit(solution)/shard_map/stack | solution.py:103
  188.5 108.7 %all-gather.2.cloned.1.call-done = bf16[4864,1792]{1,0:T(8,128)(2,1)} async-done(((bf16[304,1792]{1,0:T(8,128)(2,1)}), bf16[4864,1792]{1,0:T(8,128)(2,1)}) %all-gather.2.cloned.1.call-update) | async-done | bytes 17432592 | tf_op jit(solution)/shard_map/all_gather | solution.py:82
  297.3 12.8 %convolution_convert_fusion.1 = bf16[256,1792]{1,0:T(8,128)(2,1)} fusion(bf16[4864,1792]{1,0:T(8,128)(2,1)} %all-gather.2.cloned.1.call-done, bf16[4864,256]{1,0:T(8,128)(2,1)S(1)} %copy-done.4, pred[4864]{0:T(1024)(128)(4,1)S(1)} %get-tuple-element.35, pred[4864]{0:T(1024)(128)(4,1)S(1)} %get-tuple-element.34), kind=kOutput, calls=%fused_computation.11 | convolution fusion | flops 4465688576 | bytes 20850176 | tf_op jit(solution)/shard_map/dot_general | solution.py:84
  (21 shorter events, 0.1 us)
Async XLA Ops:
  7.2 40.9 %copy-start = (bf16[256,1792]{1,0:T(8,128)(2,1)S(1)}, bf16[256,1792]{1,0:T(8,128)(2,1)}, u32[]{:S(2)}) copy-start(bf16[256,1792]{1,0:T(8,128)(2,1)} %param.15) | copy-start | bytes 2752516
  7.2 173.3 %reduce-scatter.2.cloned.1.call-start = ((), (), s32[]{:S(2)}) async-start(), calls=%async_computation.1 | async-start | bytes 18522112 | tf_op jit(solution)/shard_map/reduce_scatter | solution.py:87
  59.8 4.6 %copy-start.5 = (s32[16]{0:T(128)S(1)}, s32[16]{0:T(128)}, u32[]{:S(2)}) copy-start(s32[16]{0:T(128)} %param.13) | copy-start | bytes 196
  59.8 237.5 %all-gather.2.cloned.1.call-start = ((), (), s32[]{:S(2)}) async-start(), calls=%async_computation.2 | async-start | bytes 18522112 | tf_op jit(solution)/shard_map/all_gather | solution.py:82
  64.4 35.9 %collective-permute-start = (bf16[3,272,1792]{2,1,0:T(8,128)(2,1)}, bf16[3,272,1792]{2,1,0:T(8,128)(2,1)}, u32[]{:S(2)}, u32[]{:S(2)}) collective-permute-start(bf16[3,272,1792]{2,1,0:T(8,128)(2,1)} %fusion.2), channel_id=1, source_target_pairs={{0,16},{16,32},{32,48},{48,64},{64,80},{80,96},{96,112},{112,0},{1... | collective-permute-start | bytes 8773640 | tf_op jit(solution)/shard_map/ppermute | solution.py:18
  104.6 2.6 copy-start.3
  107.3 11.2 %collective-permute-start.1 = (bf16[3,16,1792]{2,1,0:T(8,128)(2,1)S(1)}, bf16[3,16,1792]{2,1,0:T(8,128)(2,1)S(1)}, u32[]{:S(2)}, u32[]{:S(2)}) collective-permute-start(bf16[3,16,1792]{2,1,0:T(8,128)(2,1)S(1)} %get-tuple-element.7), channel_id=1, source_target_pairs={{0,1},{1,2},{2,3},{3,4},{4,5},{5,6},{6,7},{7,8},{8,9},{9,10},{10,1... | collective-permute-start | bytes 516104 | tf_op jit(solution)/shard_map/ppermute | solution.py:28
  111.2 11.8 %collective-permute-start.2 = (bf16[3,16,1792]{2,1,0:T(8,128)(2,1)S(1)}, bf16[3,16,1792]{2,1,0:T(8,128)(2,1)S(1)}, u32[]{:S(2)}, u32[]{:S(2)}) collective-permute-start(bf16[3,16,1792]{2,1,0:T(8,128)(2,1)S(1)} %get-tuple-element.8), channel_id=1, source_target_pairs={{1,0},{2,1},{3,2},{4,3},{5,4},{6,5},{7,6},{8,7},{9,8},{10,9},{11,1... | collective-permute-start | bytes 516104 | tf_op jit(solution)/shard_map/ppermute | solution.py:29
  123.0 6.6 %slice-start = ((s8[5849088]{0:T(1024)(128)(4,1)}), s8[4194304]{0:T(1024)(128)(4,1)S(1)}, s32[]{:S(2)}) async-start(s8[5849088]{0:T(1024)(128)(4,1)} %bitcast.83), calls=%async_computation.3 | async-start | bytes 8388608
  123.0 6.5 %slice-start.1 = ((s8[5849088]{0:T(1024)(128)(4,1)}), s8[1654784]{0:T(1024)(128)(4,1)S(1)}, s32[]{:S(2)}) async-start(s8[5849088]{0:T(1024)(128)(4,1)} %bitcast.83), calls=%async_computation.4 | async-start | bytes 3309568
  138.3 2.8 copy-start.2
  185.3 111.9 %copy-start.4 = (bf16[4864,256]{1,0:T(8,128)(2,1)S(1)}, bf16[4864,256]{1,0:T(8,128)(2,1)}, u32[]{:S(2)}) copy-start(bf16[4864,256]{1,0:T(8,128)(2,1)} %gather_fusion) | copy-start | bytes 7471108
  297.3 12.8 %copy-start.1 = (bf16[256,1792]{1,0:T(8,128)(2,1)S(1)}, bf16[256,1792]{1,0:T(8,128)(2,1)}, u32[]{:S(2)}) copy-start(bf16[256,1792]{1,0:T(8,128)(2,1)} %param.15) | copy-start | bytes 2752516
Sparse Core Ops, SparseCore 0:
  59.9 120.5 reduce-scatter.1
  182.9 114.3 all-gather.1
where the time goes:
time: 318 us; the launch traced here: 317 us
  waiting for transfers between devices  187 us (59%)
  local copies, waits for them, and re-layouts  43.7 us (14%)
  other arithmetic  37.9 us (12%)
  matrix products  24.5 us (8%)
  between operations  18.6 us (6%)
  starting transfers between devices  5.45 us (2%)
    all_gather x1, waiting for transfers between devices, body(): lax.all_gather(moved[0].astype(jnp.bfloat16), 'fsdp', axis=0, tiled=True)  109 us
    reduce_scatter x1, waiting for transfers between devices, body(): lax.psum_scatter(lax.dot_general(picked, cotangent, (((0,), (0,)), ((), (...  38.2 us
    ppermute x1, waiting for transfers between devices, passed_along(): return lax.ppermute(value, axis, pairs)  31.9 us
    gather x1, local copies, waits for them, and re-layouts, pick_columns(): picked = jnp.take(tokens, target, axis=1)  14.4 us
    dot_general x1, matrix products, body(): hidden = jnp.dot(picked, block_rows, preferred_element_type=jnp.float32)  12.8 us
    dot_general x1, matrix products, body(): lax.dot_general(picked, cotangent, (((0,), (0,)), ((), ())), preferred_el...  11.7 us
    lt x1, other arithmetic, pick_columns(): offsets < length  10.8 us
    select_n x1, other arithmetic, pick_columns(): picked = jnp.take(tokens, target, axis=1)  10.8 us
  transfers between devices with their start and end apart: 5, of which 5 were waited for; matrix products, arithmetic and copies ran while one was open for 11% of the time, Pallas kernels for 0%

commit v1 on v0

v1 whole, which is shorter than its diff:
```python
import jax
import jax.numpy as jnp
from jax import lax
from jax.experimental import pallas as pl
from jax.experimental.pallas import tpu as pltpu
from jax.sharding import PartitionSpec as P

beta_one = 0.9
beta_two = 0.95
learn_rate = 0.01
decay_rate = 0.1
epsilon = 1e-08
correct_one = 1.0 - 0.9**8
correct_two = 1.0 - 0.95**8

MESH = pl.DeviceIdType.MESH
SIDE = 4
ROWS = 256
NEAR = 8
FAR = 24
MOVE = 16
SHORT = ROWS - 2 * NEAR
OLD = ROWS + 2 * NEAR
NEW = ROWS + 2 * FAR
CUT = 256
DEPTH = 1152
TALL = 1088
W_HALF = 144
G_HALF = 160
A_HALF = 128
BF = jnp.bfloat16
F32 = jnp.float32


def rows_of(count):
    return lax.broadcasted_iota(jnp.int32, (count, CUT), 0)


def rows_from(ref, start, count):
    base = pl.multiple_of((start // 8) * 8, 8)
    rest = start - base
    tiles = ref[pl.ds(base, count + 8), :].reshape(count // 8 + 1, 8, CUT)
    turned = pltpu.roll(tiles, lax.rem(8 - rest, 8), 1)
    inner = lax.broadcasted_iota(jnp.int32, (count // 8, 8, CUT), 1)
    return jnp.where(inner < 8 - rest, turned[:-1], turned[1:]).reshape(count, CUT)


def prepare(old_bounds, failed, states, w_own, w_back, m_back, r_own, r_back, pad):
    group, member = lax.axis_index("dp"), lax.axis_index("fsdp")
    following = lax.rem(group + 1, lax.axis_size("dp"))
    lost = failed[member]
    slot = rows_of(OLD)
    for copy, owner, keep, window, rims in (
        (0, group, lost != group, w_own, r_own),
        (1, following, lost == following, w_back, r_back),
    ):
        start = old_bounds[owner, member]
        length = old_bounds[owner, member + 1] - start
        shift = start - ROWS * member + NEAR
        usable = jnp.where(keep, length, 0)
        some = rows_of(MOVE) < usable
        for state in range(3):
            value = states[state, copy]
            pad[state, MOVE : MOVE + OLD] = value
            if state == 0:
                moved = rows_from(pad.at[state], MOVE - shift, OLD)
                place = slot - shift
                window[0] = jnp.where((place >= 0) & (place < usable), moved, 0.0).astype(BF)
            elif copy == 1:
                m_back[0, state - 1] = value.astype(BF)
            rims[0, 0, state] = jnp.where(some, value[:MOVE], 0.0).astype(BF)
            rims[1, 0, state] = jnp.where(some, rows_from(pad.at[state], length, MOVE), 0.0).astype(BF)


def update(old_bounds, new_bounds, failed, states, w_back, m_back, rims, gradient, out, ext, g_pad, w_pad, r_pad):
    group, member = lax.axis_index("dp"), lax.axis_index("fsdp")
    lost = failed[member] == group
    old_start = old_bounds[group, member]
    old_len = old_bounds[group, member + 1] - old_start
    new_start = new_bounds[group, member]
    new_len = new_bounds[group, member + 1] - new_start
    step = new_start - old_start
    from_back = jnp.where(lost, old_len, 0)
    slot = rows_of(OLD)
    w_pad[:OLD] = w_back[0].astype(F32)
    moved = []
    for state in range(3):
        if state == 0:
            back = rows_from(w_pad, old_start - ROWS * member + NEAR, OLD)
        else:
            back = m_back[0, state - 1].astype(F32)
        value = jnp.where(slot < from_back, back, states[state, 0])
        r_pad[: 2 * MOVE] = jnp.zeros((2 * MOVE, CUT), F32)
        r_pad[2 * MOVE : 3 * MOVE] = rims[0, 0, state].astype(F32)
        r_pad[3 * MOVE :] = jnp.zeros((3 * MOVE + 8, CUT), F32)
        late = rows_from(r_pad, 2 * MOVE - (old_len - SHORT), 3 * MOVE)
        ext[state, :MOVE] = rims[1, 0, state].astype(F32)
        value = jnp.where(slot < old_len, value, 0.0)
        ext[state, MOVE : MOVE + SHORT] = value[:SHORT]
        ext[state, MOVE + SHORT : MOVE + OLD] = value[SHORT:] + late[: OLD - SHORT]
        ext[state, MOVE + OLD : MOVE + OLD + MOVE] = late[OLD - SHORT :]
        moved.append(rows_from(ext.at[state], MOVE + step, NEW))
    g_pad[:NEW] = gradient[0]
    grad = rows_from(g_pad, new_start - ROWS * member + FAR, NEW)
    weight, one, two = moved
    one = beta_one * one + (1.0 - beta_one) * grad
    two = beta_two * two + (1.0 - beta_two) * grad * grad
    direction = one / correct_one / (jnp.sqrt(two / correct_two) + epsilon) + decay_rate * weight
    here = rows_of(NEW) < new_len
    out[0] = jnp.where(here, weight - learn_rate * direction, 0.0)
    out[1] = jnp.where(here, one, 0.0)
    out[2] = jnp.where(here, two, 0.0)


def exchange(
    count,
    tokens, cot, w_own, w_back, m_back, r_own, r_back,
    act, grad, w_out, m_out, rims_out,
    tok, tok_t, cots, ws, wk, w_mine, w_arr, r_mine, r_arr,
    g_all, a_all, g_opp, g_opp_in, g_side, g_side_in, a_opp, a_opp_in, a_side, a_side_in, g_fin, a_fin,
    send, recv, local, tok_send, tok_recv, mate_send, mate_recv, w_send, w_recv, misc_send, misc_recv, misc_local,
):
    dp, member = lax.axis_index("dp"), lax.axis_index("fsdp")
    groups, members = lax.axis_size("dp"), lax.axis_size("fsdp")
    y, z = member // SIDE, lax.rem(member, SIDE)
    core = lax.rem(dp, 2)
    y_to = [{"fsdp": lax.rem(y + r, SIDE) * SIDE + z} for r in range(SIDE)]
    z_to = [{"fsdp": y * SIDE + lax.rem(z + r, SIDE)} for r in range(SIDE)]
    following, preceding = {"dp": lax.rem(dp + 1, groups)}, {"dp": lax.rem(dp + groups - 1, groups)}
    mate = {"dp": dp + 1 - 2 * core}
    f_up, f_down = {"fsdp": lax.rem(member + 1, members)}, {"fsdp": lax.rem(member + members - 1, members)}

    barrier = pltpu.get_barrier_semaphore()
    peers = y_to[1:] + [z_to[1], z_to[3], following, preceding, mate, f_up, f_down]
    for peer in peers:
        pl.semaphore_signal(barrier, inc=1, device_id=peer, device_id_type=MESH)
    pl.semaphore_wait(barrier, len(peers))

    def remote(src, dst, ssem, rsem, peer):
        return pltpu.make_async_remote_copy(
            src_ref=src, dst_ref=dst, send_sem=ssem, recv_sem=rsem, device_id=peer, device_id_type=MESH
        )

    def columns(c):
        return pl.ds(pl.multiple_of(c * CUT, CUT), CUT)

    half = pl.ds(pl.multiple_of(core * (ROWS // 2), ROWS // 2), ROWS // 2)
    other = pl.ds(pl.multiple_of((1 - core) * (ROWS // 2), ROWS // 2), ROWS // 2)

    def tok_copy(r):
        place = pl.ds(pl.multiple_of(lax.rem(y + r, SIDE) * (SIDE * ROWS), SIDE * ROWS), DEPTH)
        return remote(tokens.at[half, place], tok.at[SIDE - r, half], tok_send.at[r], tok_recv.at[r], y_to[r])

    def mate_copy(r):
        return remote(tok.at[SIDE - r, half], tok.at[SIDE - r, half], mate_send.at[r], mate_recv.at[r], mate)

    def w_copy(c):
        return remote(w_back.at[c], w_arr.at[c], w_send.at[c], w_recv.at[c], following)

    def misc(k):
        if k == 0:
            return remote(r_back, r_arr, misc_send.at[0], misc_recv.at[0], following)
        if k == 1:
            return remote(m_back, m_out, misc_send.at[1], misc_recv.at[1], following)
        if k == 2:
            return remote(r_mine.at[0], rims_out.at[0], misc_send.at[2], misc_recv.at[2], f_down)
        return remote(r_mine.at[1], rims_out.at[1], misc_send.at[3], misc_recv.at[3], f_up)

    def copy(kind, c):
        src, dst, peer = {
            0: (lambda: (ws.at[c, 0], ws.at[c, 3], z_to[1])),
            1: (lambda: (ws.at[c, 0], ws.at[c, 1], z_to[3])),
            2: (lambda: (ws.at[c, 3, :W_HALF], ws.at[c, 2, :W_HALF], z_to[1])),
            3: (lambda: (ws.at[c, 1, W_HALF:], ws.at[c, 2, W_HALF:], z_to[3])),
            4: (lambda: (cot.at[:, columns(c)], cots.at[c, 3], y_to[1])),
            5: (lambda: (cot.at[:, columns(c)], cots.at[c, 1], y_to[3])),
            6: (lambda: (cots.at[c, 3, :A_HALF], cots.at[c, 2, :A_HALF], y_to[1])),
            7: (lambda: (cots.at[c, 1, A_HALF:], cots.at[c, 2, A_HALF:], y_to[3])),
            8: (lambda: (g_opp.at[c, :G_HALF], g_opp_in.at[c, :G_HALF], z_to[1])),
            9: (lambda: (g_opp.at[c, G_HALF:], g_opp_in.at[c, G_HALF:], z_to[3])),
            10: (lambda: (g_side.at[c, 0], g_side_in.at[c, 0], z_to[1])),
            11: (lambda: (g_side.at[c, 1], g_side_in.at[c, 1], z_to[3])),
            12: (lambda: (a_opp.at[c, :A_HALF], a_opp_in.at[c, :A_HALF], y_to[1])),
            13: (lambda: (a_opp.at[c, A_HALF:], a_opp_in.at[c, A_HALF:], y_to[3])),
            14: (lambda: (a_side.at[c, 0], a_side_in.at[c, 0], y_to[1])),
            15: (lambda: (a_side.at[c, 1], a_side_in.at[c, 1], y_to[3])),
        }[kind]()
        return remote(src, dst, send.at[kind, c], recv.at[kind, c], peer)

    def here(k, c):
        src, dst = {
            0: (lambda: (cot.at[:, columns(c)], cots.at[c, 0])),
            1: (lambda: (g_fin.at[c], grad.at[c])),
            2: (lambda: (a_fin.at[c], act.at[:, columns(c)])),
            3: (lambda: (w_arr.at[c], w_out.at[c])),
        }[k]()
        return pltpu.make_async_copy(src, dst, local.at[k, c])

    def mine(k):
        own = pl.ds(pl.multiple_of(y * (SIDE * ROWS), SIDE * ROWS), DEPTH)
        src, dst = ((w_own, w_mine), (r_own, r_mine), (tokens.at[:, own], tok.at[0]))[k]
        return pltpu.make_async_copy(src, dst, misc_local.at[k])

    for r in (1, 3, 2):
        tok_copy(r).start()
    misc(0).start()

    @pl.loop(0, count)
    def _(c):
        w_copy(c).start()
        here(0, c).start()

    for k in range(3):
        mine(k).start()
    misc(1).start()
    wk[: 2 * NEAR] = jnp.zeros((2 * NEAR, CUT), BF)
    wk[SIDE * ROWS + 2 * MOVE :] = jnp.zeros((DEPTH - SIDE * ROWS - 2 * MOVE, CUT), BF)
    mine(0).wait()

    def gather(c):
        copy(4, c).start()
        copy(5, c).start()
        w_copy(c).wait_recv()
        here(3, c).start()
        ws[c, 0] = w_mine[c] + w_arr[c]
        copy(0, c).start()
        copy(1, c).start()

    def hand_on(c):
        for kind in (0, 1, 4, 5):
            copy(kind, c).wait_recv()
            copy(kind + 2, c).start()

    def multiply(c):
        slot = lax.rem(c, 3)
        here(0, c).wait()
        copy(6, c).wait_recv()
        copy(7, c).wait_recv()

        @pl.loop(0, TALL // OLD)
        def _(i):
            rows = pl.ds(pl.multiple_of(i * OLD, 16), OLD)
            g_all[slot, rows] = jnp.dot(
                tok_t[rows], cots[c].reshape(SIDE * ROWS, CUT), preferred_element_type=F32
            )

        far = pl.ds(pl.multiple_of(lax.rem(z + 2, SIDE) * ROWS, ROWS), NEW)
        g_opp[c] = g_all[slot, far].astype(BF)
        copy(8, c).start()
        copy(9, c).start()
        copy(2, c).wait_recv()
        copy(3, c).wait_recv()
        for p in range(SIDE):
            source = lax.rem(p - z + SIDE, SIDE)
            at = ROWS * p + MOVE
            if p == 0:
                wk[at : at + MOVE] = ws[c, source, :MOVE]
            else:
                wk[at : at + MOVE] = wk[at : at + MOVE] + ws[c, source, :MOVE]
            wk[at + MOVE : at + OLD] = ws[c, source, MOVE:]

        @pl.loop(0, SIDE)
        def _(r):
            a_all[slot, r] = jnp.dot(tok[r], wk[...], preferred_element_type=F32)

        a_opp[c] = a_all[slot, 2].astype(BF)
        copy(12, c).start()
        copy(13, c).start()

    def add_on(c):
        slot = lax.rem(c, 3)
        copy(8, c).wait_recv()
        copy(9, c).wait_recv()
        up = pl.multiple_of(lax.rem(z + 1, SIDE) * ROWS, ROWS)
        down = pl.multiple_of(lax.rem(z + 3, SIDE) * ROWS, ROWS)
        g_side[c, 0, :G_HALF] = (g_all[slot, pl.ds(up, G_HALF)] + g_opp_in[c, :G_HALF].astype(F32)).astype(BF)
        g_side[c, 0, G_HALF:] = g_all[slot, pl.ds(up + G_HALF, NEW - G_HALF)].astype(BF)
        g_side[c, 1, :G_HALF] = g_all[slot, pl.ds(down, G_HALF)].astype(BF)
        g_side[c, 1, G_HALF:] = (
            g_all[slot, pl.ds(down + G_HALF, NEW - G_HALF)] + g_opp_in[c, G_HALF:].astype(F32)
        ).astype(BF)
        copy(10, c).start()
        copy(11, c).start()
        copy(12, c).wait_recv()
        copy(13, c).wait_recv()
        a_side[c, 0, :A_HALF] = (a_all[slot, 1, :A_HALF] + a_opp_in[c, :A_HALF].astype(F32)).astype(BF)
        a_side[c, 0, A_HALF:] = a_all[slot, 1, A_HALF:].astype(BF)
        a_side[c, 1, :A_HALF] = a_all[slot, 3, :A_HALF].astype(BF)
        a_side[c, 1, A_HALF:] = (a_all[slot, 3, A_HALF:] + a_opp_in[c, A_HALF:].astype(F32)).astype(BF)
        copy(14, c).start()
        copy(15, c).start()

    def finish(c):
        slot = lax.rem(c, 3)
        copy(10, c).wait_recv()
        copy(11, c).wait_recv()
        rows = pl.ds(pl.multiple_of(z * ROWS, ROWS), NEW)
        g_fin[c] = g_all[slot, rows] + g_side_in[c, 0].astype(F32) + g_side_in[c, 1].astype(F32)
        here(1, c).start()
        copy(14, c).wait_recv()
        copy(15, c).wait_recv()
        a_fin[c] = (a_all[slot, 0] + a_side_in[c, 0].astype(F32) + a_side_in[c, 1].astype(F32)).astype(BF)
        here(2, c).start()

    gather(0)
    for r in (1, 3, 2):
        tok_copy(r).wait_recv()
        mate_copy(r).start()
    gather(1)
    hand_on(0)

    mine(1).wait()
    misc(0).wait_recv()
    r_mine[...] = r_mine[...] + r_arr[...]
    misc(2).start()
    misc(3).start()

    mine(2).wait()
    tok_t[:, :ROWS] = tok[0].T
    for r in (1, 3, 2):
        mate_copy(r).wait_recv()
        k = SIDE - r
        tok_t[:, ROWS * k : ROWS * (k + 1)] = tok[k].T

    @pl.loop(2, count + 4)
    def _(t):
        @pl.when(t < count)
        def _():
            gather(t)

        @pl.when(t < count + 1)
        def _():
            hand_on(t - 1)

        @pl.when((t >= 3) & (t < count + 3))
        def _():
            add_on(t - 3)

        @pl.when(t < count + 2)
        def _():
            multiply(t - 2)

        @pl.when(t >= 4)
        def _():
            finish(t - 4)

    @pl.loop(0, count)
    def _(c):
        for kind in range(16):
            copy(kind, c).wait_send()
        w_copy(c).wait_send()
        for k in (1, 2, 3):
            here(k, c).wait()

    for r in (1, 2, 3):
        tok_copy(r).wait_send()
        mate_copy(r).wait_send()
    misc(0).wait_send()
    for k in (1, 2, 3):
        misc(k).wait()


def body(old_states, old_bounds, new_bounds, failed, tokens, cotangent):
    width = cotangent.shape[1]
    count = width // CUT
    smem = pl.BlockSpec(memory_space=pltpu.SMEM)
    hbm = pl.BlockSpec(memory_space=pl.ANY)
    shape = jax.ShapeDtypeStruct
    wide = shape((count, OLD, CUT), BF)
    two_wide = shape((count, 2, OLD, CUT), BF)
    rim = shape((2, count, 3, MOVE, CUT), BF)
    wide_spec = pl.BlockSpec((1, OLD, CUT), lambda i: (i, 0, 0))
    two_spec = pl.BlockSpec((1, 2, OLD, CUT), lambda i: (i, 0, 0, 0))
    rim_spec = pl.BlockSpec((2, 1, 3, MOVE, CUT), lambda i: (0, i, 0, 0, 0))

    w_own, w_back, m_back, r_own, r_back = pl.pallas_call(
        prepare,
        grid=(count,),
        in_specs=[smem, smem, pl.BlockSpec((3, 2, OLD, CUT), lambda i: (0, 0, 0, i))],
        out_specs=[wide_spec, wide_spec, two_spec, rim_spec, rim_spec],
        out_shape=[wide, wide, two_wide, rim, rim],
        scratch_shapes=[pltpu.VMEM((3, OLD + 2 * MOVE + 8, CUT), F32)],
        name="prepare",
    )(old_bounds, failed, old_states)

    padded = jnp.pad(tokens, ((0, 0), (FAR, DEPTH - SIDE * ROWS - FAR)))
    vm = pltpu.VMEM
    dma = pltpu.SemaphoreType.DMA
    act, grad, w_arr, m_arr, rims = pl.pallas_call(
        lambda *refs: exchange(count, *refs),
        in_specs=[hbm] * 7,
        out_specs=[hbm] * 5,
        out_shape=[
            shape((ROWS, width), BF),
            shape((count, NEW, CUT), F32),
            wide,
            two_wide,
            rim,
        ],
        scratch_shapes=[
            vm((SIDE, ROWS, DEPTH), BF),
            vm((DEPTH, SIDE * ROWS), BF),
            vm((count, SIDE, ROWS, CUT), BF),
            vm((count, SIDE, OLD, CUT), BF),
            vm((DEPTH, CUT), BF),
            vm((count, OLD, CUT), BF),
            vm((count, OLD, CUT), BF),
            vm((2, count, 3, MOVE, CUT), BF),
            vm((2, count, 3, MOVE, CUT), BF),
            vm((3, TALL, CUT), F32),
            vm((3, SIDE, ROWS, CUT), F32),
            vm((count, NEW, CUT), BF),
            vm((count, NEW, CUT), BF),
            vm((count, 2, NEW, CUT), BF),
            vm((count, 2, NEW, CUT), BF),
            vm((count, ROWS, CUT), BF),
            vm((count, ROWS, CUT), BF),
            vm((count, 2, ROWS, CUT), BF),
            vm((count, 2, ROWS, CUT), BF),
            vm((count, NEW, CUT), F32),
            vm((count, ROWS, CUT), BF),
            dma((16, count)),
            dma((16, count)),
            dma((4, count)),
            dma((SIDE,)),
            dma((SIDE,)),
            dma((SIDE,)),
            dma((SIDE,)),
            dma((count,)),
            dma((count,)),
            dma((4,)),
            dma((4,)),
            dma((3,)),
        ],
        compiler_params=pltpu.CompilerParams(
            collective_id=0, has_side_effects=True, vmem_limit_bytes=50 * 2**20
        ),
        name="exchange",
    )(padded, cotangent, w_own, w_back, m_back, r_own, r_back)

    new_states = pl.pallas_call(
        update,
        grid=(count,),
        in_specs=[
            smem,
            smem,
            smem,
            pl.BlockSpec((3, 1, OLD, CUT), lambda i: (0, 0, 0, i)),
            wide_spec,
            two_spec,
            rim_spec,
            pl.BlockSpec((1, NEW, CUT), lambda i: (i, 0, 0)),
        ],
        out_specs=pl.BlockSpec((3, NEW, CUT), lambda i: (0, 0, i)),
        out_shape=shape((3, NEW, width), F32),
        scratch_shapes=[
            vm((3, NEW + 2 * MOVE + 8, CUT), F32),
            vm((NEW + 2 * FAR + 8, CUT), F32),
            vm((OLD + MOVE + 8, CUT), F32),
            vm((6 * MOVE + 8, CUT), F32),
        ],
        name="update",
    )(old_bounds, new_bounds, failed, old_states, w_arr, m_arr, rims, grad)
    return new_states, act


def solution(mesh):
    in_specs = (
        P(None, None, ("dp", "fsdp"), None),
        P(),
        P(),
        P(),
        P("fsdp", None),
        P("fsdp", "dp"),
    )
    out_specs = (P(None, ("dp", "fsdp"), None), P("fsdp", "dp"))
    return jax.shard_map(body, mesh=mesh, in_specs=in_specs, out_specs=out_specs, check_vma=False)
```

time: 318 us -> 129 us (0.41)
  waiting for transfers between devices: 187 us -> 0 us
  Pallas kernels: 0 us -> 118 us
  other arithmetic: 37.9 us -> 0 us
  local copies, waits for them, and re-layouts: 43.7 us -> 8.3 us
  matrix products: 24.5 us -> 0 us
  between operations: 18.6 us -> 0.66 us
  starting transfers between devices: 5.45 us -> 0 us
    pallas_call x0 -> x3, Pallas kernels: none -> 118 us  [the longest x1 97.8 us: body(): pl.pallas_call(lambda *refs: exchange(count, *refs), in_specs=[hbm] * 7,...]
    all_gather x1 -> x0, waiting for transfers between devices: 109 us -> none  [body(): lax.all_gather(moved[0].astype(jnp.bfloat16), 'fsdp', axis=0, tiled=True)]
    ppermute x3 -> x0, waiting for transfers between devices: 39.7 us -> none  [the longest x1 31.9 us: passed_along(): return lax.ppermute(value, axis, pairs)]
    reduce_scatter x1 -> x0, waiting for transfers between devices: 38.2 us -> none  [body(): lax.psum_scatter(lax.dot_general(picked, cotangent, (((0,), (0,)), ((), (...]
    dot_general x2 -> x0, matrix products: 24.5 us -> none  [the longest x1 12.8 us: body(): hidden = jnp.dot(picked, block_rows, preferred_element_type=jnp.float32)]
    select_n x3 -> x0, other arithmetic: 19 us -> none  [the longest x1 10.8 us: pick_columns(): picked = jnp.take(tokens, target, axis=1)]
    gather x2 -> x0, local copies, waits for them, and re-layouts: 15.1 us -> none  [the longest x1 14.4 us: pick_columns(): picked = jnp.take(tokens, target, axis=1)]
    dynamic_update_slice x3 -> x0, local copies, waits for them, and re-layouts: 11.5 us -> none  [the longest x1 6.51 us: body(): extended = lax.dynamic_update_slice_in_dim(extended, from_left, 0, 1)]
  transfers between devices with their start and end apart: 5 -> 0, of which waited for: 5 -> 0; matrix products, arithmetic and copies ran while one was open for 11% -> 0% of each run, Pallas kernels for 0% -> 0%
where the time goes in v1:
time: 129 us; the launch traced here: 127 us
  Pallas kernels  118 us (91%)
  local copies, waits for them, and re-layouts  8.3 us (6%)
    pallas_call x1, Pallas kernels, body(): pl.pallas_call(lambda *refs: exchange(count, *refs), in_specs=[hbm] * 7,...  97.8 us
    pallas_call x1, Pallas kernels, body(): pl.pallas_call(update, grid=(count,), in_specs=[smem, smem, smem, pl.Bloc...  11.2 us
    pallas_call x1, Pallas kernels, body(): pl.pallas_call(prepare, grid=(count,), in_specs=[smem, smem, pl.BlockSpec...  9.26 us
    unnamed x11, local copies, waits for them, and re-layouts  4.57 us
    pad x1, local copies, waits for them, and re-layouts, body(): padded = jnp.pad(tokens, ((0, 0), (FAR, DEPTH - SIDE * ROWS - FAR)))  3.73 us

profile of v1, /device:TPU:0, one launch (start us, length us, event | category | flops | bytes accessed | tf_op | source)
XLA Modules:
  0.0 127.2 jit_solution(7020143190984429819)
XLA Ops:
  0.6 3.7 %pad.4.refs_0_ = bf16[256,4224]{1,0:T(8,128)(2,1)} pad(bf16[256,4096]{1,0:T(8,128)(2,1)} %param.10, bf16[]{:T(256)} %constant.2.clone.1), padding=0_0x24_104 | pad | bytes 4259842 | tf_op jit(solution)/shard_map/jit(_pad)/pad | solution.py:386
  4.4 0.0 copy-start.1
  4.4 9.3 %prepare.1 = (bf16[7,272,256]{2,1,0:T(8,128)(2,1)}, bf16[7,272,256]{2,1,0:T(8,128)(2,1)}, bf16[7,2,272,256]{3,2,1,0:T(8,128)(2,1)}, bf16[2,7,3,16,256]{4,3,2,1,0:T(8,128)(2,1)}, bf16[2,7,3,16,256]{4,3,2,1,0:T(8,128)(2,1)}) custom-call(s32[8,17]{1,0:T(8,128)} %old_bounds.3, s32[16]{0:T(128)} %failed.3, f32[3,2,272,1792]{3,2,1,0:T(8,128)} %states.3), custom_call_target="tpu_custom_call" | custom-call | tf_op jit(solution)/shard_map/prepare/pallas_call | solution.py:376
  13.6 0.0 copy-done.1
  13.6 0.0 copy-start.3
  13.6 1.0 copy-done.3
  14.6 0.0 copy-start.4
  14.6 1.0 copy-done.4
  15.6 97.8 %exchange.1 = (bf16[256,1792]{1,0:T(8,128)(2,1)S(1)}, f32[7,304,256]{2,1,0:T(8,128)}, bf16[7,272,256]{2,1,0:T(8,128)(2,1)S(1)}, bf16[7,2,272,256]{3,2,1,0:T(8,128)(2,1)}, bf16[2,7,3,16,256]{4,3,2,1,0:T(8,128)(2,1)S(1)}) custom-call(bf16[256,4224]{1,0:T(8,128)(2,1)} %pad.4.refs_0_, bf16[256,1792]{1,0:T(8,128)(2,1)S(1)} %copy-done.1, ...), custom_call_target="tpu_custom_call" | custom-call | tf_op jit(solution)/shard_map/exchange/pallas_call | solution.py:389
  113.4 0.0 copy-start
  113.4 1.0 copy-done
  114.4 0.0 copy-start.2
  114.4 0.7 copy-done.2
  115.1 11.2 %update.1 = f32[3,304,1792]{2,1,0:T(8,128)} custom-call(s32[8,17]{1,0:T(8,128)} %old_bounds.3, s32[8,17]{1,0:T(8,128)} %new_bounds.1, s32[16]{0:T(128)} %failed.3, f32[3,2,272,1792]{3,2,1,0:T(8,128)} %states.3, bf16[7,272,256]{2,1,0:T(8,128)(2,1)} %copy-done, bf16[7,2,272,256]{3,2,1,0:T(8,128)(2,1)} %get-tuple-element.18.m_back, ...), custom_call_target="tpu_custom_call" | custom-call | tf_op jit(solution)/shard_map/update/pallas_call | solution.py:441
  126.3 0.9 copy.9
Async XLA Ops:
  4.4 9.3 %copy-start.1 = (bf16[256,1792]{1,0:T(8,128)(2,1)S(1)}, bf16[256,1792]{1,0:T(8,128)(2,1)}, u32[]{:S(2)}) copy-start(bf16[256,1792]{1,0:T(8,128)(2,1)} %refs_1_.1) | copy-start | bytes 2752516
  13.6 1.0 copy-start.3
  14.6 1.0 copy-start.4
  113.4 1.0 copy-start
  114.4 0.7 copy-start.2

commit v2 on v1

v2 whole, which is shorter than its diff:
```python
import jax
import jax.numpy as jnp
from jax import lax
from jax.experimental import pallas as pl
from jax.experimental.pallas import tpu as pltpu
from jax.sharding import PartitionSpec as P

beta_one = 0.9
beta_two = 0.95
learn_rate = 0.01
decay_rate = 0.1
epsilon = 1e-08
correct_one = 1.0 - 0.9**8
correct_two = 1.0 - 0.95**8

MESH = pl.DeviceIdType.MESH
SIDE = 4
ROWS = 256
NEAR = 8
FAR = 24
MOVE = 16
SHORT = ROWS - 2 * NEAR
OLD = ROWS + 2 * NEAR
NEW = ROWS + 2 * FAR
CUT = 256
SPARE = 64
LANE = 128
DEPTH = SIDE * ROWS + 2 * LANE
SKIP = 96
TALL = 1088
W_HALF = 144
G_HALF = 160
A_HALF = 128
PRE = 5
AHEAD = 3
HAND = 1
MOM = 1
ADD = 2
END = 4
LOAD = 2
RING = END + 1
BF = jnp.bfloat16
F32 = jnp.float32


def rows_of(count):
    return lax.broadcasted_iota(jnp.int32, (count, CUT), 0)


def rows_from(ref, start, count, coarse):
    tiles = ref[: count + 8 + sum(coarse), :].reshape(count // 8 + 1 + sum(coarse) // 8, 8, CUT)
    amount = jnp.broadcast_to(start, (1, 8, CUT))
    for bit in coarse:
        tiles = jnp.where((amount & bit) > 0, tiles[bit // 8 :], tiles[: -(bit // 8)])
    for bit in (1, 2, 4):
        tiles = jnp.where((amount & bit) > 0, pltpu.roll(tiles, 8 - bit, 1), tiles)
    inner = lax.broadcasted_iota(jnp.int32, (1, 8, CUT), 1)
    return jnp.where(inner < 8 - (amount & 7), tiles[:-1], tiles[1:]).reshape(count, CUT)


def exchange(
    count,
    old_bounds, new_bounds, failed, states, tokens, cot,
    new_states, act,
    w_in, m_in, ext, e_head, e_tail,
    tok, tok_t, cots, ws, wk_wide, wk, w_mine, w_back, w_arr, m_back, m_arr, r_mine, r_back, r_arr, rims,
    g_all, a_all, g_opp, g_opp_in, g_side, g_side_in, a_opp, a_opp_in, a_side, a_side_in, a_fin, out, g_pad, w_pad, r_pad,
    send, recv, local, tok_send, tok_recv, mate_send, mate_recv, dp_send, dp_recv, misc_send, misc_recv, misc_local,
):
    dp, member = lax.axis_index("dp"), lax.axis_index("fsdp")
    groups, members = lax.axis_size("dp"), lax.axis_size("fsdp")
    y, z = member // SIDE, lax.rem(member, SIDE)
    core = lax.rem(dp, 2)
    y_to = [{"fsdp": lax.rem(y + r, SIDE) * SIDE + z} for r in range(SIDE)]
    z_to = [{"fsdp": y * SIDE + lax.rem(z + r, SIDE)} for r in range(SIDE)]
    next_group = lax.rem(dp + 1, groups)
    following, preceding = {"dp": next_group}, {"dp": lax.rem(dp + groups - 1, groups)}
    mate = {"dp": dp + 1 - 2 * core}
    f_up, f_down = {"fsdp": lax.rem(member + 1, members)}, {"fsdp": lax.rem(member + members - 1, members)}

    barrier = pltpu.get_barrier_semaphore()
    peers = y_to[1:] + [z_to[1], z_to[3], following, preceding, mate, f_up, f_down]
    for peer in peers:
        pl.semaphore_signal(barrier, inc=1, device_id=peer, device_id_type=MESH)

    def remote(src, dst, ssem, rsem, peer):
        return pltpu.make_async_remote_copy(
            src_ref=src, dst_ref=dst, send_sem=ssem, recv_sem=rsem, device_id=peer, device_id_type=MESH
        )

    def columns(c):
        return pl.ds(pl.multiple_of(c * CUT, CUT), CUT)

    half = pl.ds(pl.multiple_of(core * (ROWS // 2), ROWS // 2), ROWS // 2)

    def parts(owner):
        span = SIDE * ROWS
        whole = span * SIDE
        begin = pl.multiple_of(owner * span, span)
        before = pl.multiple_of(lax.rem(owner * span + whole - LANE, whole), LANE)
        after = pl.multiple_of(lax.rem(owner * span + span, whole), LANE)
        return (
            (pl.ds(begin, span), pl.ds(LANE, span)),
            (pl.ds(before, LANE), pl.ds(0, LANE)),
            (pl.ds(after, LANE), pl.ds(LANE + span, LANE)),
        )

    def tok_copy(r, k):
        source, target = parts(lax.rem(y + r, SIDE))[k]
        return remote(
            tokens.at[half, source], tok.at[SIDE - r, half, target], tok_send.at[r, k], tok_recv.at[r, k], y_to[r]
        )

    def mate_copy(r):
        return remote(tok.at[SIDE - r, half], tok.at[SIDE - r, half], mate_send.at[r], mate_recv.at[r], mate)

    def w_copy(c):
        return remote(w_back.at[c], w_arr.at[c], dp_send.at[0, c], dp_recv.at[0, c], following)

    def m_copy(c):
        return remote(m_back.at[c], m_arr.at[c], dp_send.at[1, c], dp_recv.at[1, c], following)

    def rim_copy(k):
        if k == 0:
            return remote(r_back, r_arr, misc_send.at[0], misc_recv.at[0], following)
        if k == 1:
            return remote(r_mine.at[0], rims.at[0], misc_send.at[1], misc_recv.at[1], f_down)
        return remote(r_mine.at[1], rims.at[1], misc_send.at[2], misc_recv.at[2], f_up)

    def copy(kind, c):
        src, dst, peer = {
            0: (lambda: (ws.at[c, 0], ws.at[c, 3], z_to[1])),
            1: (lambda: (ws.at[c, 0], ws.at[c, 1], z_to[3])),
            2: (lambda: (ws.at[c, 3, :W_HALF], ws.at[c, 2, :W_HALF], z_to[1])),
            3: (lambda: (ws.at[c, 1, W_HALF:], ws.at[c, 2, W_HALF:], z_to[3])),
            4: (lambda: (cot.at[:, columns(c)], cots.at[c, 3], y_to[1])),
            5: (lambda: (cot.at[:, columns(c)], cots.at[c, 1], y_to[3])),
            6: (lambda: (cots.at[c, 3, :A_HALF], cots.at[c, 2, :A_HALF], y_to[1])),
            7: (lambda: (cots.at[c, 1, A_HALF:], cots.at[c, 2, A_HALF:], y_to[3])),
            8: (lambda: (g_opp.at[c, :G_HALF], g_opp_in.at[c, :G_HALF], z_to[1])),
            9: (lambda: (g_opp.at[c, G_HALF:], g_opp_in.at[c, G_HALF:], z_to[3])),
            10: (lambda: (g_side.at[c, 0], g_side_in.at[c, 0], z_to[1])),
            11: (lambda: (g_side.at[c, 1], g_side_in.at[c, 1], z_to[3])),
            12: (lambda: (a_opp.at[c, :A_HALF], a_opp_in.at[c, :A_HALF], y_to[1])),
            13: (lambda: (a_opp.at[c, A_HALF:], a_opp_in.at[c, A_HALF:], y_to[3])),
            14: (lambda: (a_side.at[c, 0], a_side_in.at[c, 0], y_to[1])),
            15: (lambda: (a_side.at[c, 1], a_side_in.at[c, 1], y_to[3])),
        }[kind]()
        return remote(src, dst, send.at[kind, c], recv.at[kind, c], peer)

    def here(k, c):
        src, dst = {
            0: (lambda: (cot.at[:, columns(c)], cots.at[c, 0])),
            1: (lambda: (states.at[0, :, :, columns(c)], w_in.at[lax.rem(c, 3), :, MOVE : MOVE + OLD])),
            2: (lambda: (states.at[1:3, 1, :, columns(c)], m_in.at[lax.rem(c, 2)])),
            3: (lambda: (states.at[:, 0, :, columns(c)], ext.at[lax.rem(c, 3), :, MOVE : MOVE + OLD])),
            4: (lambda: (a_fin.at[c], act.at[:, columns(c)])),
            5: (lambda: (out.at[lax.rem(c, 3)], new_states.at[:, :, columns(c)])),
        }[k]()
        return pltpu.make_async_copy(src, dst, local.at[k, c])

    def mine(k):
        if k < 3:
            source, target = parts(y)[k]
            src, dst = tokens.at[:, source], tok.at[0, :, target]
        elif k == 3:
            src, dst = states.at[:, :, :MOVE], e_head
        else:
            src, dst = states.at[:, :, OLD - 3 * MOVE :], e_tail.at[:, :, : 3 * MOVE]
        return pltpu.make_async_copy(src, dst, misc_local.at[k])

    lost_group = failed[member]
    old_start = old_bounds[dp, member]
    old_len = old_bounds[dp, member + 1] - old_start
    new_start = new_bounds[dp, member]
    new_len = new_bounds[dp, member + 1] - new_start
    back_start = old_bounds[next_group, member]
    back_len = old_bounds[next_group, member + 1] - back_start
    mean_start = ROWS * member
    lost_use = old_len * (lost_group == dp).astype(jnp.int32)
    own_use = old_len - lost_use
    back_use = back_len * (lost_group == next_group).astype(jnp.int32)

    def window(ref, start, usable):
        shift = start - mean_start + NEAR
        place = rows_of(OLD) - shift
        return jnp.where((place >= 0) & (place < usable), rows_from(ref, MOVE - shift, OLD, (16, 8)), 0.0).astype(BF)

    def windows(c):
        slot = lax.rem(c, 3)
        here(1, c).wait()
        w_back[c] = window(w_in.at[slot, 1], back_start, back_use)
        w_copy(c).start()
        w_mine[c] = window(w_in.at[slot, 0], old_start, own_use)

        @pl.when(c + 3 < count)
        def _():
            here(1, c + 3).start()

    def rim_rows():
        mine(3).wait()
        mine(4).wait()
        row = rows_of(MOVE)

        @pl.loop(0, count)
        def _(c):
            for number, (length, usable, rim) in enumerate(((old_len, own_use, r_mine), (back_len, back_use, r_back))):
                some = row < usable
                for state in range(3):
                    head = e_head[state, number, :, columns(c)]
                    tail = rows_from(e_tail.at[state, number, :, columns(c)], length - SHORT, MOVE, (32, 16, 8))
                    rim[0, c, state] = jnp.where(some, head, 0.0).astype(BF)
                    rim[1, c, state] = jnp.where(some, tail, 0.0).astype(BF)

    def moments(c):
        here(2, c).wait()
        m_back[c] = m_in[lax.rem(c, 2)].astype(BF)
        m_copy(c).start()

        @pl.when(c + 2 < count)
        def _():
            here(2, c + 2).start()

    def gather(c):
        copy(4, c).start()
        copy(5, c).start()
        w_copy(c).wait_recv()
        ws[c, 0] = w_mine[c] + w_arr[c]
        copy(0, c).start()
        copy(1, c).start()

    def hand_on(c):
        for kind in (0, 1, 4, 5):
            copy(kind, c).wait_recv()
            copy(kind + 2, c).start()

    def multiply(c):
        slot = lax.rem(c, RING)
        here(0, c).wait()
        copy(6, c).wait_recv()
        copy(7, c).wait_recv()

        @pl.loop(0, TALL // OLD)
        def _(i):
            rows = pl.ds(pl.multiple_of(i * OLD, 16), OLD)
            taken = pl.ds(pl.multiple_of(i * OLD + SKIP, 16), OLD)
            g_all[slot, rows] = jnp.dot(
                tok_t[taken], cots[c].reshape(SIDE * ROWS, CUT), preferred_element_type=F32
            )

        far = pl.ds(pl.multiple_of(lax.rem(z + 2, SIDE) * ROWS + NEAR, NEAR), NEW)
        g_opp[c] = g_all[slot, far].astype(BF)
        copy(8, c).start()
        copy(9, c).start()
        copy(2, c).wait_recv()
        copy(3, c).wait_recv()
        for p in range(SIDE):
            source = lax.rem(p - z + SIDE, SIDE)
            at = LANE - NEAR + ROWS * p
            piece = ws[c, source].astype(F32)
            if p == 0:
                wk_wide[at : at + MOVE] = piece[:MOVE]
            else:
                wk_wide[at : at + MOVE] = wk_wide[at : at + MOVE] + piece[:MOVE]
            wk_wide[at + MOVE : at + OLD] = piece[MOVE:]
        wk[...] = wk_wide[...].astype(BF)

        @pl.loop(0, SIDE)
        def _(r):
            a_all[slot, r] = jnp.dot(tok[r], wk[...], preferred_element_type=F32)

        a_opp[c] = a_all[slot, 2].astype(BF)
        copy(12, c).start()
        copy(13, c).start()

    def add_on(c):
        slot = lax.rem(c, RING)
        copy(8, c).wait_recv()
        copy(9, c).wait_recv()
        up = pl.multiple_of(lax.rem(z + 1, SIDE) * ROWS + NEAR, NEAR)
        down = pl.multiple_of(lax.rem(z + 3, SIDE) * ROWS + NEAR, NEAR)
        g_side[c, 0, :G_HALF] = (g_all[slot, pl.ds(up, G_HALF)] + g_opp_in[c, :G_HALF].astype(F32)).astype(BF)
        g_side[c, 0, G_HALF:] = g_all[slot, pl.ds(up + G_HALF, NEW - G_HALF)].astype(BF)
        g_side[c, 1, :G_HALF] = g_all[slot, pl.ds(down, G_HALF)].astype(BF)
        g_side[c, 1, G_HALF:] = (
            g_all[slot, pl.ds(down + G_HALF, NEW - G_HALF)] + g_opp_in[c, G_HALF:].astype(F32)
        ).astype(BF)
        copy(10, c).start()
        copy(11, c).start()
        copy(12, c).wait_recv()
        copy(13, c).wait_recv()
        a_side[c, 0, :A_HALF] = (a_all[slot, 1, :A_HALF] + a_opp_in[c, :A_HALF].astype(F32)).astype(BF)
        a_side[c, 0, A_HALF:] = a_all[slot, 1, A_HALF:].astype(BF)
        a_side[c, 1, :A_HALF] = a_all[slot, 3, :A_HALF].astype(BF)
        a_side[c, 1, A_HALF:] = (a_all[slot, 3, A_HALF:] + a_opp_in[c, A_HALF:].astype(F32)).astype(BF)
        copy(14, c).start()
        copy(15, c).start()

    def finish(c):
        slot = lax.rem(c, RING)
        at = lax.rem(c, 3)
        row = rows_of(OLD)
        here(3, c).wait()
        m_copy(c).wait_recv()
        w_pad[:OLD] = w_arr[c].astype(F32)
        moved = []
        for state in range(3):
            if state == 0:
                back = rows_from(w_pad, old_start - mean_start + NEAR, OLD, (16, 8))
            else:
                back = m_arr[c, state - 1].astype(F32)
            r_pad[2 * MOVE : 3 * MOVE] = rims[0, c, state].astype(F32)
            late = rows_from(r_pad, 2 * MOVE - (old_len - SHORT), 3 * MOVE, (32, 16, 8))
            value = jnp.where(row < lost_use, back, ext[at, state, MOVE : MOVE + OLD])
            value = jnp.where(row < old_len, value, 0.0)
            ext[at, state, :MOVE] = rims[1, c, state].astype(F32)
            ext[at, state, MOVE : MOVE + SHORT] = value[:SHORT]
            ext[at, state, MOVE + SHORT : MOVE + OLD] = value[SHORT:] + late[: OLD - SHORT]
            ext[at, state, MOVE + OLD : MOVE + OLD + MOVE] = late[OLD - SHORT :]
            moved.append(rows_from(ext.at[at, state], MOVE + new_start - old_start, NEW, (32, 16, 8)))
        copy(14, c).wait_recv()
        copy(15, c).wait_recv()
        a_fin[c] = (a_all[slot, 0] + a_side_in[c, 0].astype(F32) + a_side_in[c, 1].astype(F32)).astype(BF)
        here(4, c).start()
        copy(10, c).wait_recv()
        copy(11, c).wait_recv()
        rows = pl.ds(pl.multiple_of(z * ROWS + NEAR, NEAR), NEW)
        g_pad[:NEW] = g_all[slot, rows] + g_side_in[c, 0].astype(F32) + g_side_in[c, 1].astype(F32)
        grad = rows_from(g_pad, new_start - mean_start + FAR, NEW, (32, 16, 8))
        weight, one, two = moved
        one = beta_one * one + (1.0 - beta_one) * grad
        two = beta_two * two + (1.0 - beta_two) * grad * grad
        direction = one / correct_one / (jnp.sqrt(two / correct_two) + epsilon) + decay_rate * weight
        inside = rows_of(NEW) < new_len

        @pl.when(c >= 3)
        def _():
            here(5, c - 3).wait()

        out[at, 0] = jnp.where(inside, weight - learn_rate * direction, 0.0)
        out[at, 1] = jnp.where(inside, one, 0.0)
        out[at, 2] = jnp.where(inside, two, 0.0)
        here(5, c).start()

    for c in range(3):
        here(1, c).start()
    for k in range(5):
        mine(k).start()
    for c in range(2):
        here(2, c).start()

    @pl.loop(0, count)
    def _(c):
        here(0, c).start()

    wk_wide[:LANE] = jnp.zeros((LANE, CUT), F32)
    wk_wide[LANE + SIDE * ROWS :] = jnp.zeros((LANE, CUT), F32)
    r_pad[...] = jnp.zeros(r_pad.shape, F32)
    pl.semaphore_wait(barrier, len(peers))
    for r in (1, 3, 2):
        for k in range(3):
            tok_copy(r, k).start()
    first = -PRE

    @pl.loop(0, count + END + PRE)
    def _(step):
        t = step + first

        @pl.when(t + PRE < count)
        def _():
            windows(t + PRE)

        @pl.when((t + AHEAD >= 0) & (t + AHEAD < count))
        def _():
            gather(t + AHEAD)

        @pl.when(t == -AHEAD)
        def _():
            rim_rows()
            rim_copy(0).start()

        @pl.when(t == 1 - AHEAD)
        def _():
            for r in (1, 3, 2):
                for k in range(3):
                    tok_copy(r, k).wait_recv()
                mate_copy(r).start()

        @pl.when((t + HAND >= 0) & (t + HAND < count))
        def _():
            hand_on(t + HAND)

        @pl.when((t + MOM >= 0) & (t + MOM < count))
        def _():
            moments(t + MOM)

        @pl.when(t == -1)
        def _():
            rim_copy(0).wait_recv()
            r_mine[...] = r_mine[...] + r_arr[...]
            rim_copy(1).start()
            rim_copy(2).start()
            for k in range(3):
                mine(k).wait()
            tok_t[:, :ROWS] = tok[0].T
            for r in (1, 3, 2):
                mate_copy(r).wait_recv()
                k = SIDE - r
                tok_t[:, ROWS * k : ROWS * (k + 1)] = tok[k].T

        @pl.when((t >= ADD) & (t < count + ADD))
        def _():
            add_on(t - ADD)

        @pl.when((t >= 0) & (t < count))
        def _():
            multiply(t)

        @pl.when((t >= END - LOAD) & (t < count + END - LOAD))
        def _():
            here(3, t - END + LOAD).start()

        @pl.when(t == END)
        def _():
            rim_copy(1).wait_recv()
            rim_copy(2).wait_recv()

        @pl.when(t >= END)
        def _():
            finish(t - END)

    @pl.loop(0, count)
    def _(c):
        for kind in range(16):
            copy(kind, c).wait_send()
        w_copy(c).wait_send()
        m_copy(c).wait_send()
        here(4, c).wait()

    for c in range(count - 3, count):
        here(5, c).wait()
    for r in (1, 2, 3):
        for k in range(3):
            tok_copy(r, k).wait_send()
        mate_copy(r).wait_send()
    for k in range(3):
        rim_copy(k).wait_send()


def body(old_states, old_bounds, new_bounds, failed, tokens, cotangent):
    width = cotangent.shape[1]
    count = width // CUT
    smem = pl.BlockSpec(memory_space=pltpu.SMEM)
    hbm = pl.BlockSpec(memory_space=pl.ANY)
    shape = jax.ShapeDtypeStruct
    vm = pltpu.VMEM
    dma = pltpu.SemaphoreType.DMA
    new_states, act = pl.pallas_call(
        lambda *refs: exchange(count, *refs),
        in_specs=[smem, smem, smem, hbm, hbm, hbm],
        out_specs=[hbm, hbm],
        out_shape=[shape((3, NEW, width), F32), shape((ROWS, width), BF)],
        scratch_shapes=[
            vm((3, 2, OLD + 2 * MOVE + 8, CUT), F32),
            vm((2, 2, OLD, CUT), F32),
            vm((3, 3, NEW + SPARE, CUT), F32),
            vm((3, 2, MOVE, width), F32),
            vm((3, 2, MOVE + SPARE, width), F32),
            vm((SIDE, ROWS, DEPTH), BF),
            vm((DEPTH, SIDE * ROWS), BF),
            vm((count, SIDE, ROWS, CUT), BF),
            vm((count, SIDE, OLD, CUT), BF),
            vm((DEPTH, CUT), F32),
            vm((DEPTH, CUT), BF),
            vm((count, OLD, CUT), BF),
            vm((count, OLD, CUT), BF),
            vm((count, OLD, CUT), BF),
            vm((count, 2, OLD, CUT), BF),
            vm((count, 2, OLD, CUT), BF),
            vm((2, count, 3, MOVE, CUT), BF),
            vm((2, count, 3, MOVE, CUT), BF),
            vm((2, count, 3, MOVE, CUT), BF),
            vm((2, count, 3, MOVE, CUT), BF),
            vm((RING, TALL, CUT), F32),
            vm((RING, SIDE, ROWS, CUT), F32),
            vm((count, NEW, CUT), BF),
            vm((count, NEW, CUT), BF),
            vm((count, 2, NEW, CUT), BF),
            vm((count, 2, NEW, CUT), BF),
            vm((count, ROWS, CUT), BF),
            vm((count, ROWS, CUT), BF),
            vm((count, 2, ROWS, CUT), BF),
            vm((count, 2, ROWS, CUT), BF),
            vm((count, ROWS, CUT), BF),
            vm((3, 3, NEW, CUT), F32),
            vm((NEW + SPARE, CUT), F32),
            vm((OLD + SPARE, CUT), F32),
            vm((3 * MOVE + SPARE, CUT), F32),
            dma((16, count)),
            dma((16, count)),
            dma((6, count)),
            dma((SIDE, 3)),
            dma((SIDE, 3)),
            dma((SIDE,)),
            dma((SIDE,)),
            dma((2, count)),
            dma((2, count)),
            dma((3,)),
            dma((3,)),
            dma((5,)),
        ],
        compiler_params=pltpu.CompilerParams(
            collective_id=0, has_side_effects=True, vmem_limit_bytes=60 * 2**20
        ),
        name="exchange",
    )(old_bounds, new_bounds, failed, old_states, tokens, cotangent)
    return new_states, act


def solution(mesh):
    in_specs = (
        P(None, None, ("dp", "fsdp"), None),
        P(),
        P(),
        P(),
        P("fsdp", None),
        P("fsdp", "dp"),
    )
    out_specs = (P(None, ("dp", "fsdp"), None), P("fsdp", "dp"))
    return jax.shard_map(body, mesh=mesh, in_specs=in_specs, out_specs=out_specs, check_vma=False)
```

time: 129 us -> 104 us (0.81); the launches traced: 127 us -> 104 us
  Pallas kernels: 118 us -> 96 us
    pallas_call x3 -> x1, Pallas kernels: 118 us -> 96 us  [body(): pl.pallas_call(lambda *refs: exchange(count, *refs), in_specs=[smem, smem...]
    pad x1 -> x0, local copies, waits for them, and re-layouts: 3.73 us -> none  [body(): padded = jnp.pad(tokens, ((0, 0), (FAR, DEPTH - SIDE * ROWS - FAR)))]
    unnamed x11 -> x4, local copies, waits for them, and re-layouts: 4.57 us -> 7.07 us
where the time goes in v2:
time: 104 us
  Pallas kernels  96 us (92%)
  local copies, waits for them, and re-layouts  7.07 us (7%)
    pallas_call x1, Pallas kernels, body(): pl.pallas_call(lambda *refs: exchange(count, *refs), in_specs=[smem, smem...  96 us
    unnamed x4, local copies, waits for them, and re-layouts  7.07 us

profile of v2, /device:TPU:0, one launch (start us, length us, event | category | flops | bytes accessed | tf_op | source)
XLA Modules:
  0.0 103.7 jit_solution(6449498391345997996)
XLA Ops:
  0.6 96.0 %exchange.1 = (f32[3,304,1792]{2,1,0:T(8,128)}, bf16[256,1792]{1,0:T(8,128)(2,1)}) custom-call(s32[8,17]{1,0:T(8,128)} %refs_0_.1, s32[8,17]{1,0:T(8,128)} %refs_1_.1, s32[16]{0:T(128)} %refs_2_.1, f32[3,2,272,1792]{3,2,1,0:T(8,128)} %refs_3_.1, bf16[256,4096]{1,0:T(8,128)(2,1)} %refs_4_.1, bf16[256,1792]{1,0:T(8,128)(2,1)} %refs_5_.1), custom_call_target="tpu_custom_call" | custom-call | tf_op jit(solution)/shard_map/exchange/pallas_call | solution.py:458
  96.6 0.0 copy-start
  96.6 6.1 %copy.10 = f32[3,304,1792]{2,1,0:T(8,128)} copy(f32[3,304,1792]{2,1,0:T(8,128)} %get-tuple-element.4) | data formatting | bytes 13074432
  102.7 0.0 copy-done
  102.8 0.9 copy.11
Async XLA Ops:
  96.6 6.2 %copy-start = (bf16[256,1792]{1,0:T(8,128)(2,1)S(1)}, bf16[256,1792]{1,0:T(8,128)(2,1)}, u32[]{:S(2)}) copy-start(bf16[256,1792]{1,0:T(8,128)(2,1)} %get-tuple-element.5) | copy-start | bytes 2752516

commit v3 on v2

--- a/solution.py
+++ b/solution.py
@@ -31,10 +31,13 @@
 W_HALF = 144
 G_HALF = 160
 A_HALF = 128
-PRE = 5
-AHEAD = 3
-HAND = 1
+PRE = 7
+AHEAD = 5
+HAND = 2
 MOM = 1
+TOK_ONE = -3
+TOK_TWO = -1
+TOK_END = 0
 ADD = 2
 END = 4
 LOAD = 2
@@ -65,12 +68,13 @@
     w_in, m_in, ext, e_head, e_tail,
     tok, tok_t, cots, ws, wk_wide, wk, w_mine, w_back, w_arr, m_back, m_arr, r_mine, r_back, r_arr, rims,
     g_all, a_all, g_opp, g_opp_in, g_side, g_side_in, a_opp, a_opp_in, a_side, a_side_in, a_fin, out, g_pad, w_pad, r_pad,
-    send, recv, local, tok_send, tok_recv, mate_send, mate_recv, dp_send, dp_recv, misc_send, misc_recv, misc_local,
+    send, recv, local, tok_send, tok_recv, x_send, x_recv, mate_send, mate_recv, dp_send, dp_recv, misc_send, misc_recv, misc_local,
 ):
     dp, member = lax.axis_index("dp"), lax.axis_index("fsdp")
     groups, members = lax.axis_size("dp"), lax.axis_size("fsdp")
     y, z = member // SIDE, lax.rem(member, SIDE)
-    core = lax.rem(dp, 2)
+    x, core = dp // 2, lax.rem(dp, 2)
+    x_to = [{"dp": lax.rem(x + r, SIDE) * 2 + core} for r in range(SIDE)]
     y_to = [{"fsdp": lax.rem(y + r, SIDE) * SIDE + z} for r in range(SIDE)]
     z_to = [{"fsdp": y * SIDE + lax.rem(z + r, SIDE)} for r in range(SIDE)]
     next_group = lax.rem(dp + 1, groups)
@@ -79,7 +83,7 @@
     f_up, f_down = {"fsdp": lax.rem(member + 1, members)}, {"fsdp": lax.rem(member + members - 1, members)}
 
     barrier = pltpu.get_barrier_semaphore()
-    peers = y_to[1:] + [z_to[1], z_to[3], following, preceding, mate, f_up, f_down]
+    peers = [x_to[1], x_to[3]] + y_to[1:] + [z_to[1], z_to[3], following, preceding, mate, f_up, f_down]
     for peer in peers:
         pl.semaphore_signal(barrier, inc=1, device_id=peer, device_id_type=MESH)
 
@@ -91,7 +95,14 @@
     def columns(c):
         return pl.ds(pl.multiple_of(c * CUT, CUT), CUT)
 
-    half = pl.ds(pl.multiple_of(core * (ROWS // 2), ROWS // 2), ROWS // 2)
+    share = ROWS // 8
+    even = lax.rem(x, 2)
+
+    def rows_at(pair, part):
+        begin = (pair * 2 + core) * (2 * share)
+        if part is None:
+            return pl.ds(pl.multiple_of(begin, 2 * share), 2 * share)
+        return pl.ds(pl.multiple_of(begin + part * share, share), share)
 
     def parts(owner):
         span = SIDE * ROWS
@@ -108,11 +119,18 @@
     def tok_copy(r, k):
         source, target = parts(lax.rem(y + r, SIDE))[k]
         return remote(
-            tokens.at[half, source], tok.at[SIDE - r, half, target], tok_send.at[r, k], tok_recv.at[r, k], y_to[r]
+            tokens.at[rows_at(even, None), source], tok.at[SIDE - r, rows_at(even, None), target], tok_send.at[r, k], tok_recv.at[r, k], y_to[r]
         )
 
-    def mate_copy(r):
-        return remote(tok.at[SIDE - r, half], tok.at[SIDE - r, half], mate_send.at[r], mate_recv.at[r], mate)
+    def x_copy(k, part):
+        rows = rows_at(even, part)
+        return remote(
+            tok.at[k, rows], tok.at[k, rows], x_send.at[k, part], x_recv.at[k, part], x_to[1 if part == 0 else 3]
+        )
+
+    def mate_copy(k, near):
+        rows = rows_at(even if near == 0 else 1 - even, None)
+        return remote(tok.at[k, rows], tok.at[k, rows], mate_send.at[k, near], mate_recv.at[k, near], mate)
 
     def w_copy(c):
         return remote(w_back.at[c], w_arr.at[c], dp_send.at[0, c], dp_recv.at[0, c], following)
@@ -379,12 +397,14 @@
             rim_rows()
             rim_copy(0).start()
 
-        @pl.when(t == 1 - AHEAD)
+        @pl.when(t == TOK_ONE)
         def _():
             for r in (1, 3, 2):
                 for k in range(3):
                     tok_copy(r, k).wait_recv()
-                mate_copy(r).start()
+                x_copy(SIDE - r, 0).start()
+                x_copy(SIDE - r, 1).start()
+                mate_copy(SIDE - r, 0).start()
 
         @pl.when((t + HAND >= 0) & (t + HAND < count))
         def _():
@@ -400,12 +420,22 @@
             r_mine[...] = r_mine[...] + r_arr[...]
             rim_copy(1).start()
             rim_copy(2).start()
+
+        @pl.when(t == TOK_TWO)
+        def _():
             for k in range(3):
                 mine(k).wait()
             tok_t[:, :ROWS] = tok[0].T
-            for r in (1, 3, 2):
-                mate_copy(r).wait_recv()
-                k = SIDE - r
+            for k in (3, 1, 2):
+                x_copy(k, 0).wait_recv()
+                x_copy(k, 1).wait_recv()
+                mate_copy(k, 1).start()
+
+        @pl.when(t == TOK_END)
+        def _():
+            for k in (3, 1, 2):
+                mate_copy(k, 0).wait_recv()
+                mate_copy(k, 1).wait_recv()
                 tok_t[:, ROWS * k : ROWS * (k + 1)] = tok[k].T
 
         @pl.when((t >= ADD) & (t < count + ADD))
@@ -442,7 +472,9 @@
     for r in (1, 2, 3):
         for k in range(3):
             tok_copy(r, k).wait_send()
-        mate_copy(r).wait_send()
+        for k in range(2):
+            x_copy(r, k).wait_send()
+            mate_copy(r, k).wait_send()
     for k in range(3):
         rim_copy(k).wait_send()
 
@@ -501,8 +533,10 @@
             dma((6, count)),
             dma((SIDE, 3)),
             dma((SIDE, 3)),
-            dma((SIDE,)),
-            dma((SIDE,)),
+            dma((SIDE, 2)),
+            dma((SIDE, 2)),
+            dma((SIDE, 2)),
+            dma((SIDE, 2)),
             dma((2, count)),
             dma((2, count)),
             dma((3,)),

time: 104 us -> 95.3 us (0.916)
  Pallas kernels: 96 us -> 87.4 us
    pallas_call x1, Pallas kernels: 96 us -> 87.4 us  [body(): pl.pallas_call(lambda *refs: exchange(count, *refs), in_specs=[smem, smem...]
where the time goes in v3:
time: 95.3 us; the launch traced here: 95.1 us
  Pallas kernels  87.4 us (92%)
  local copies, waits for them, and re-layouts  7.07 us (7%)
    pallas_call x1, Pallas kernels, body(): pl.pallas_call(lambda *refs: exchange(count, *refs), in_specs=[smem, smem...  87.4 us
    unnamed x4, local copies, waits for them, and re-layouts  7.07 us

profile of v3, /device:TPU:0, one launch (start us, length us, event | category | flops | bytes accessed | tf_op | source)
XLA Modules:
  0.0 95.1 jit_solution(761318820061247400)
XLA Ops:
  0.6 87.4 %exchange.1 = (f32[3,304,1792]{2,1,0:T(8,128)}, bf16[256,1792]{1,0:T(8,128)(2,1)}) custom-call(s32[8,17]{1,0:T(8,128)} %refs_0_.1, s32[8,17]{1,0:T(8,128)} %refs_1_.1, s32[16]{0:T(128)} %refs_2_.1, f32[3,2,272,1792]{3,2,1,0:T(8,128)} %refs_3_.1, bf16[256,4096]{1,0:T(8,128)(2,1)} %refs_4_.1, bf16[256,1792]{1,0:T(8,128)(2,1)} %refs_5_.1), custom_call_target="tpu_custom_call" | custom-call | tf_op jit(solution)/shard_map/exchange/pallas_call | solution.py:490
  88.1 0.0 copy-start
  88.1 6.1 %copy.10 = f32[3,304,1792]{2,1,0:T(8,128)} copy(f32[3,304,1792]{2,1,0:T(8,128)} %get-tuple-element.4) | data formatting | bytes 13074432
  94.2 0.0 copy-done
  94.2 0.9 copy.11
Async XLA Ops:
  88.1 6.2 %copy-start = (bf16[256,1792]{1,0:T(8,128)(2,1)S(1)}, bf16[256,1792]{1,0:T(8,128)(2,1)}, u32[]{:S(2)}) copy-start(bf16[256,1792]{1,0:T(8,128)(2,1)} %get-tuple-element.5) | copy-start | bytes 2752516

commit v4 on v3

--- a/solution.py
+++ b/solution.py
@@ -40,7 +40,7 @@
 TOK_END = 0
 ADD = 2
 END = 4
-LOAD = 2
+LOAD = 1
 RING = END + 1
 BF = jnp.bfloat16
 F32 = jnp.float32
@@ -67,7 +67,7 @@
     new_states, act,
     w_in, m_in, ext, e_head, e_tail,
     tok, tok_t, cots, ws, wk_wide, wk, w_mine, w_back, w_arr, m_back, m_arr, r_mine, r_back, r_arr, rims,
-    g_all, a_all, g_opp, g_opp_in, g_side, g_side_in, a_opp, a_opp_in, a_side, a_side_in, a_fin, out, g_pad, w_pad, r_pad,
+    g_all, a_all, g_opp, g_opp_in, g_side, g_side_in, a_opp, a_opp_in, a_side, a_side_in, g_pad, w_pad, r_pad,
     send, recv, local, tok_send, tok_recv, x_send, x_recv, mate_send, mate_recv, dp_send, dp_recv, misc_send, misc_recv, misc_local,
 ):
     dp, member = lax.axis_index("dp"), lax.axis_index("fsdp")
@@ -136,7 +136,7 @@
         return remote(w_back.at[c], w_arr.at[c], dp_send.at[0, c], dp_recv.at[0, c], following)
 
     def m_copy(c):
-        return remote(m_back.at[c], m_arr.at[c], dp_send.at[1, c], dp_recv.at[1, c], following)
+        return remote(m_back.at[lax.rem(c, 4)], m_arr.at[c], dp_send.at[1, c], dp_recv.at[1, c], following)
 
     def rim_copy(k):
         if k == 0:
@@ -171,9 +171,7 @@
             0: (lambda: (cot.at[:, columns(c)], cots.at[c, 0])),
             1: (lambda: (states.at[0, :, :, columns(c)], w_in.at[lax.rem(c, 3), :, MOVE : MOVE + OLD])),
             2: (lambda: (states.at[1:3, 1, :, columns(c)], m_in.at[lax.rem(c, 2)])),
-            3: (lambda: (states.at[:, 0, :, columns(c)], ext.at[lax.rem(c, 3), :, MOVE : MOVE + OLD])),
-            4: (lambda: (a_fin.at[c], act.at[:, columns(c)])),
-            5: (lambda: (out.at[lax.rem(c, 3)], new_states.at[:, :, columns(c)])),
+            3: (lambda: (states.at[:, 0, :, columns(c)], ext.at[lax.rem(c, 2), :, MOVE : MOVE + OLD])),
         }[k]()
         return pltpu.make_async_copy(src, dst, local.at[k, c])
 
@@ -204,12 +202,19 @@
         place = rows_of(OLD) - shift
         return jnp.where((place >= 0) & (place < usable), rows_from(ref, MOVE - shift, OLD, (16, 8)), 0.0).astype(BF)
 
+    def back_window(c):
+        here(1, c).wait()
+        w_back[c] = window(w_in.at[lax.rem(c, 3), 1], back_start, back_use)
+
     def windows(c):
         slot = lax.rem(c, 3)
-        here(1, c).wait()
-        w_back[c] = window(w_in.at[slot, 1], back_start, back_use)
-        w_copy(c).start()
-        w_mine[c] = window(w_in.at[slot, 0], old_start, own_use)
+
+        @pl.when(c > 0)
+        def _():
+            back_window(c)
+            w_copy(c).start()
+
+        w_mine[lax.rem(c, 4)] = window(w_in.at[slot, 0], old_start, own_use)
 
         @pl.when(c + 3 < count)
         def _():
@@ -232,7 +237,12 @@
 
     def moments(c):
         here(2, c).wait()
-        m_back[c] = m_in[lax.rem(c, 2)].astype(BF)
+
+        @pl.when(c >= 4)
+        def _():
+            m_copy(c - 4).wait_send()
+
+        m_back[lax.rem(c, 4)] = m_in[lax.rem(c, 2)].astype(BF)
         m_copy(c).start()
 
         @pl.when(c + 2 < count)
@@ -243,7 +253,7 @@
         copy(4, c).start()
         copy(5, c).start()
         w_copy(c).wait_recv()
-        ws[c, 0] = w_mine[c] + w_arr[c]
+        ws[c, 0] = w_mine[lax.rem(c, 4)] + w_arr[c]
         copy(0, c).start()
         copy(1, c).start()
 
@@ -283,13 +293,13 @@
             wk_wide[at + MOVE : at + OLD] = piece[MOVE:]
         wk[...] = wk_wide[...].astype(BF)
 
-        @pl.loop(0, SIDE)
-        def _(r):
-            a_all[slot, r] = jnp.dot(tok[r], wk[...], preferred_element_type=F32)
-
-        a_opp[c] = a_all[slot, 2].astype(BF)
+        a_opp[c] = jnp.dot(tok[2], wk[...], preferred_element_type=F32).astype(BF)
         copy(12, c).start()
         copy(13, c).start()
+
+        @pl.loop(0, 3)
+        def _(k):
+            a_all[slot, k] = jnp.dot(tok[k + k // 2], wk[...], preferred_element_type=F32)
 
     def add_on(c):
         slot = lax.rem(c, RING)
@@ -309,14 +319,14 @@
         copy(13, c).wait_recv()
         a_side[c, 0, :A_HALF] = (a_all[slot, 1, :A_HALF] + a_opp_in[c, :A_HALF].astype(F32)).astype(BF)
         a_side[c, 0, A_HALF:] = a_all[slot, 1, A_HALF:].astype(BF)
-        a_side[c, 1, :A_HALF] = a_all[slot, 3, :A_HALF].astype(BF)
-        a_side[c, 1, A_HALF:] = (a_all[slot, 3, A_HALF:] + a_opp_in[c, A_HALF:].astype(F32)).astype(BF)
+        a_side[c, 1, :A_HALF] = a_all[slot, 2, :A_HALF].astype(BF)
+        a_side[c, 1, A_HALF:] = (a_all[slot, 2, A_HALF:] + a_opp_in[c, A_HALF:].astype(F32)).astype(BF)
         copy(14, c).start()
         copy(15, c).start()
 
     def finish(c):
         slot = lax.rem(c, RING)
-        at = lax.rem(c, 3)
+        at = lax.rem(c, 2)
         row = rows_of(OLD)
         here(3, c).wait()
         m_copy(c).wait_recv()
@@ -338,8 +348,7 @@
             moved.append(rows_from(ext.at[at, state], MOVE + new_start - old_start, NEW, (32, 16, 8)))
         copy(14, c).wait_recv()
         copy(15, c).wait_recv()
-        a_fin[c] = (a_all[slot, 0] + a_side_in[c, 0].astype(F32) + a_side_in[c, 1].astype(F32)).astype(BF)
-        here(4, c).start()
+        act[:, columns(c)] = (a_all[slot, 0] + a_side_in[c, 0].astype(F32) + a_side_in[c, 1].astype(F32)).astype(BF)
         copy(10, c).wait_recv()
         copy(11, c).wait_recv()
         rows = pl.ds(pl.multiple_of(z * ROWS + NEAR, NEAR), NEW)
@@ -351,14 +360,9 @@
         direction = one / correct_one / (jnp.sqrt(two / correct_two) + epsilon) + decay_rate * weight
         inside = rows_of(NEW) < new_len
 
-        @pl.when(c >= 3)
-        def _():
-            here(5, c - 3).wait()
-
-        out[at, 0] = jnp.where(inside, weight - learn_rate * direction, 0.0)
-        out[at, 1] = jnp.where(inside, one, 0.0)
-        out[at, 2] = jnp.where(inside, two, 0.0)
-        here(5, c).start()
+        new_states[0, :, columns(c)] = jnp.where(inside, weight - learn_rate * direction, 0.0)
+        new_states[1, :, columns(c)] = jnp.where(inside, one, 0.0)
+        new_states[2, :, columns(c)] = jnp.where(inside, two, 0.0)
 
     for c in range(3):
         here(1, c).start()
@@ -374,10 +378,12 @@
     wk_wide[:LANE] = jnp.zeros((LANE, CUT), F32)
     wk_wide[LANE + SIDE * ROWS :] = jnp.zeros((LANE, CUT), F32)
     r_pad[...] = jnp.zeros(r_pad.shape, F32)
+    back_window(0)
     pl.semaphore_wait(barrier, len(peers))
     for r in (1, 3, 2):
         for k in range(3):
             tok_copy(r, k).start()
+    w_copy(0).start()
     first = -PRE
 
     @pl.loop(0, count + END + PRE)
@@ -464,11 +470,9 @@
         for kind in range(16):
             copy(kind, c).wait_send()
         w_copy(c).wait_send()
+
+    for c in range(count - 4, count):
         m_copy(c).wait_send()
-        here(4, c).wait()
-
-    for c in range(count - 3, count):
-        here(5, c).wait()
     for r in (1, 2, 3):
         for k in range(3):
             tok_copy(r, k).wait_send()
@@ -490,12 +494,12 @@
     new_states, act = pl.pallas_call(
         lambda *refs: exchange(count, *refs),
         in_specs=[smem, smem, smem, hbm, hbm, hbm],
-        out_specs=[hbm, hbm],
-        out_shape=[shape((3, NEW, width), F32), shape((ROWS, width), BF)],
+        out_specs=[pl.BlockSpec(memory_space=vm)] * 2,
+        out_shape=[vm((3, NEW, width), F32), vm((ROWS, width), BF)],
         scratch_shapes=[
             vm((3, 2, OLD + 2 * MOVE + 8, CUT), F32),
             vm((2, 2, OLD, CUT), F32),
-            vm((3, 3, NEW + SPARE, CUT), F32),
+            vm((2, 3, NEW + SPARE, CUT), F32),
             vm((3, 2, MOVE, width), F32),
             vm((3, 2, MOVE + SPARE, width), F32),
             vm((SIDE, ROWS, DEPTH), BF),
@@ -504,17 +508,17 @@
             vm((count, SIDE, OLD, CUT), BF),
             vm((DEPTH, CUT), F32),
             vm((DEPTH, CUT), BF),
+            vm((4, OLD, CUT), BF),
             vm((count, OLD, CUT), BF),
             vm((count, OLD, CUT), BF),
-            vm((count, OLD, CUT), BF),
-            vm((count, 2, OLD, CUT), BF),
+            vm((4, 2, OLD, CUT), BF),
             vm((count, 2, OLD, CUT), BF),
             vm((2, count, 3, MOVE, CUT), BF),
             vm((2, count, 3, MOVE, CUT), BF),
             vm((2, count, 3, MOVE, CUT), BF),
             vm((2, count, 3, MOVE, CUT), BF),
             vm((RING, TALL, CUT), F32),
-            vm((RING, SIDE, ROWS, CUT), F32),
+            vm((RING, 3, ROWS, CUT), F32),
             vm((count, NEW, CUT), BF),
             vm((count, NEW, CUT), BF),
             vm((count, 2, NEW, CUT), BF),
@@ -523,14 +527,12 @@
             vm((count, ROWS, CUT), BF),
             vm((count, 2, ROWS, CUT), BF),
             vm((count, 2, ROWS, CUT), BF),
-            vm((count, ROWS, CUT), BF),
-            vm((3, 3, NEW, CUT), F32),
             vm((NEW + SPARE, CUT), F32),
             vm((OLD + SPARE, CUT), F32),
             vm((3 * MOVE + SPARE, CUT), F32),
             dma((16, count)),
             dma((16, count)),
-            dma((6, count)),
+            dma((4, count)),
             dma((SIDE, 3)),
             dma((SIDE, 3)),
             dma((SIDE, 2)),
@@ -544,7 +546,7 @@
             dma((5,)),
         ],
         compiler_params=pltpu.CompilerParams(
-            collective_id=0, has_side_effects=True, vmem_limit_bytes=60 * 2**20
+            collective_id=0, has_side_effects=True, vmem_limit_bytes=54 * 2**20
         ),
         name="exchange",
     )(old_bounds, new_bounds, failed, old_states, tokens, cotangent)

time: 95.3 us -> 90.7 us (0.952)
  local copies, waits for them, and re-layouts: 7.07 us -> 3.71 us
  Pallas kernels: 87.4 us -> 86.2 us
    unnamed x4 -> x2, local copies, waits for them, and re-layouts: 7.07 us -> 3.71 us
    pallas_call x1, Pallas kernels: 87.4 us -> 86.2 us  [body(): pl.pallas_call(lambda *refs: exchange(count, *refs), in_specs=[smem, smem...]
where the time goes in v4:
time: 90.7 us; the launch traced here: 90.6 us
  Pallas kernels  86.2 us (95%)
  local copies, waits for them, and re-layouts  3.71 us (4%)
    pallas_call x1, Pallas kernels, body(): pl.pallas_call(lambda *refs: exchange(count, *refs), in_specs=[smem, smem...  86.2 us
    unnamed x2, local copies, waits for them, and re-layouts  3.71 us

profile of v4, /device:TPU:0, one launch (start us, length us, event | category | flops | bytes accessed | tf_op | source)
XLA Modules:
  0.0 90.6 jit_solution(5167363939619067102)
XLA Ops:
  0.6 86.2 %exchange.1 = (f32[3,304,1792]{2,1,0:T(8,128)S(1)}, bf16[256,1792]{1,0:T(8,128)(2,1)S(1)}) custom-call(s32[8,17]{1,0:T(8,128)} %refs_0_.1, s32[8,17]{1,0:T(8,128)} %refs_1_.1, s32[16]{0:T(128)} %refs_2_.1, f32[3,2,272,1792]{3,2,1,0:T(8,128)} %refs_3_.1, bf16[256,4096]{1,0:T(8,128)(2,1)} %refs_4_.1, bf16[256,1792]{1,0:T(8,128)(2,1)} %refs_5_.1), custom_call_target="tpu_custom_call" | custom-call | tf_op jit(solution)/shard_map/exchange/pallas_call | solution.py:494
  86.9 2.8 %copy.10 = f32[3,304,1792]{2,1,0:T(8,128)} copy(f32[3,304,1792]{2,1,0:T(8,128)S(1)} %get-tuple-element.2) | data formatting | bytes 13074432
  89.7 0.9 %copy.11 = bf16[256,1792]{1,0:T(8,128)(2,1)} copy(bf16[256,1792]{1,0:T(8,128)(2,1)S(1)} %get-tuple-element.3) | data formatting | bytes 1835008

commit v5 on v4

--- a/solution.py
+++ b/solution.py
@@ -28,7 +28,7 @@
 DEPTH = SIDE * ROWS + 2 * LANE
 SKIP = 96
 TALL = 1088
-W_HALF = 144
+W_HALF = 128
 G_HALF = 160
 A_HALF = 128
 PRE = 7
@@ -444,13 +444,13 @@
                 mate_copy(k, 1).wait_recv()
                 tok_t[:, ROWS * k : ROWS * (k + 1)] = tok[k].T
 
+        @pl.when((t >= 0) & (t < count))
+        def _():
+            multiply(t)
+
         @pl.when((t >= ADD) & (t < count + ADD))
         def _():
             add_on(t - ADD)
-
-        @pl.when((t >= 0) & (t < count))
-        def _():
-            multiply(t)
 
         @pl.when((t >= END - LOAD) & (t < count + END - LOAD))
         def _():

time: 90.7 us -> 89.7 us (0.989)
  Pallas kernels: 86.2 us -> 85.2 us
    pallas_call x1, Pallas kernels: 86.2 us -> 85.2 us  [body(): pl.pallas_call(lambda *refs: exchange(count, *refs), in_specs=[smem, smem...]
where the time goes in v5:
time: 89.7 us; the launch traced here: 89.5 us
  Pallas kernels  85.2 us (95%)
  local copies, waits for them, and re-layouts  3.71 us (4%)
    pallas_call x1, Pallas kernels, body(): pl.pallas_call(lambda *refs: exchange(count, *refs), in_specs=[smem, smem...  85.2 us
    unnamed x2, local copies, waits for them, and re-layouts  3.71 us

profile of v5, /device:TPU:0, one launch (start us, length us, event | category | flops | bytes accessed | tf_op | source)
XLA Modules:
  0.0 89.5 jit_solution(10588275474439803860)
XLA Ops:
  0.6 85.2 %exchange.1 = (f32[3,304,1792]{2,1,0:T(8,128)S(1)}, bf16[256,1792]{1,0:T(8,128)(2,1)S(1)}) custom-call(s32[8,17]{1,0:T(8,128)} %refs_0_.1, s32[8,17]{1,0:T(8,128)} %refs_1_.1, s32[16]{0:T(128)} %refs_2_.1, f32[3,2,272,1792]{3,2,1,0:T(8,128)} %refs_3_.1, bf16[256,4096]{1,0:T(8,128)(2,1)} %refs_4_.1, bf16[256,1792]{1,0:T(8,128)(2,1)} %refs_5_.1), custom_call_target="tpu_custom_call" | custom-call | tf_op jit(solution)/shard_map/exchange/pallas_call | solution.py:494
  85.8 2.8 %copy.10 = f32[3,304,1792]{2,1,0:T(8,128)} copy(f32[3,304,1792]{2,1,0:T(8,128)S(1)} %get-tuple-element.2) | data formatting | bytes 13074432
  88.6 0.9 %copy.11 = bf16[256,1792]{1,0:T(8,128)(2,1)} copy(bf16[256,1792]{1,0:T(8,128)(2,1)S(1)} %get-tuple-element.3) | data formatting | bytes 1835008

commit v6 on v5

--- a/solution.py
+++ b/solution.py
@@ -39,7 +39,7 @@
 TOK_TWO = -1
 TOK_END = 0
 ADD = 2
-END = 4
+END = 3
 LOAD = 1
 RING = END + 1
 BF = jnp.bfloat16

time: 89.7 us -> 91 us (1.014)
  Pallas kernels: 85.2 us -> 86.6 us
    pallas_call x1, Pallas kernels: 85.2 us -> 86.6 us  [body(): pl.pallas_call(lambda *refs: exchange(count, *refs), in_specs=[smem, smem...]
where the time goes in v6:
time: 91 us; the launch traced here: 90.9 us
  Pallas kernels  86.6 us (95%)
  local copies, waits for them, and re-layouts  3.71 us (4%)
    pallas_call x1, Pallas kernels, body(): pl.pallas_call(lambda *refs: exchange(count, *refs), in_specs=[smem, smem...  86.6 us
    unnamed x2, local copies, waits for them, and re-layouts  3.71 us

profile of v6, /device:TPU:0, one launch (start us, length us, event | category | flops | bytes accessed | tf_op | source)
XLA Modules:
  0.0 90.9 jit_solution(2434728385314146969)
XLA Ops:
  0.6 86.6 %exchange.1 = (f32[3,304,1792]{2,1,0:T(8,128)S(1)}, bf16[256,1792]{1,0:T(8,128)(2,1)S(1)}) custom-call(s32[8,17]{1,0:T(8,128)} %refs_0_.1, s32[8,17]{1,0:T(8,128)} %refs_1_.1, s32[16]{0:T(128)} %refs_2_.1, f32[3,2,272,1792]{3,2,1,0:T(8,128)} %refs_3_.1, bf16[256,4096]{1,0:T(8,128)(2,1)} %refs_4_.1, bf16[256,1792]{1,0:T(8,128)(2,1)} %refs_5_.1), custom_call_target="tpu_custom_call" | custom-call | tf_op jit(solution)/shard_map/exchange/pallas_call | solution.py:494
  87.2 2.8 %copy.10 = f32[3,304,1792]{2,1,0:T(8,128)} copy(f32[3,304,1792]{2,1,0:T(8,128)S(1)} %get-tuple-element.2) | data formatting | bytes 13074432
  90.0 0.9 %copy.11 = bf16[256,1792]{1,0:T(8,128)(2,1)} copy(bf16[256,1792]{1,0:T(8,128)(2,1)S(1)} %get-tuple-element.3) | data formatting | bytes 1835008
